TPU v7x, 32 devices: a whole 2x2x4 slice. The times are simulated.
32 devices in a mesh: date: 2 (over y), trade: 8 (over z, x), path: 2 (over core).
Axes of the slice: x: 2, y: 2, z: 4, core: 2. Of those that a mesh axis runs over, the one named last changes fastest.
Arguments:
- basis_values: bfloat16 [2048, 512], P(('date', 'path')), parts along dimension 0, may hold values from -6 to 6
- coefficients: bfloat16 [2560, 512], P(('date', 'trade')), parts along dimension 0, may hold values from -0.25 to 0.25
- trade_cpty: int32 [1280], P('trade'), may hold values from 0 to 127, as said below
- trade_bucket: int32 [1280], P('trade'), may hold values from 0 to 127
- risk_weights: float32 [128], replicated, may hold values from 0.5 to 2
- correlation: float32 [128, 128], replicated, may hold values from 0 to 1, as said below
- funding_spread: float32 [128], P('trade'), may hold values from 0.5 to 2
Outputs:
- margin: float32 [128, 2048], P('trade', ('date', 'path')), parts along dimension 1
- basis_adjoint: bfloat16 [2048, 512], P(('date', 'path')), parts along dimension 0
There are 2 independent parts, one for each index of `date`. A program takes and returns all parts, laid end to end along the dimension named above; an argument that names none is the same for every part. Nothing has to cross between parts.
Inputs may be any that keep to these rules, and one draw needn't show every extreme that they name: `trade_cpty`: counterparty c belongs to owner block c // 16. Among the trades of one device, at most 40 belong to counterparties of one owner block; in every draw one owner block receives exactly 40 from every device. Counterparties differ in size. `correlation`: symmetric positive definite with unit diagonal; smallest eigenvalue at least 0.01; entries positive.
All inputs are finite; a program needn't handle non-finite values.
Results may differ from a plain program's by a relative error of at most 0.0034.
Values may be sent and summed in bfloat16 or wider, within the bound.
No kernel may reach another device: no remote copies, remote signals or barrier semaphores. Data moves between devices by JAX's collectives and lax.ppermute only.
A program may use at most 64 MiB of HBM per device.

v0:
```python
import jax
import jax.numpy as jnp
from jax import lax
from jax.sharding import PartitionSpec as P


def margin_terms(arrived, got_codes, risk_weights, correlation, funding_spread):
    path_rows = arrived.shape[0]
    cpty_count = funding_spread.shape[0]
    bucket_count = risk_weights.shape[0]
    is_filled = got_codes >= 0
    column_ids = jnp.arange(cpty_count * bucket_count, dtype=jnp.int32)
    hot_table = (got_codes[:, None] == column_ids[None, :]).astype(jnp.bfloat16)
    bucket_sums = jnp.dot(arrived, hot_table, preferred_element_type=jnp.float32)
    weighted = (
        bucket_sums.reshape(path_rows, cpty_count, bucket_count) * risk_weights[None, None, :]
    )
    rho_w = jnp.einsum("pcb,db->pcd", weighted, correlation, precision=lax.Precision.HIGHEST)
    margin_now = jnp.sqrt(jnp.sum(weighted * rho_w, axis=2) + 1e-06)
    sens_bar = (
        funding_spread[None, :, None] * risk_weights[None, None, :] * rho_w / margin_now[:, :, None]
    )
    flat_bar = sens_bar.reshape(path_rows, cpty_count * bucket_count)
    safe_codes = jnp.where(is_filled, got_codes, 0)
    slot_bar = jnp.take(flat_bar, safe_codes, axis=1) * is_filled[None, :].astype(jnp.float32)
    return (margin_now, slot_bar.astype(jnp.bfloat16))


def body(
    basis_values, coefficients, trade_cpty, trade_bucket, risk_weights, correlation, funding_spread
):
    owners = lax.axis_size("trade")
    per_device = coefficients.shape[0]
    capacity = max(2, 2 * per_device // owners)
    slot_total = owners * capacity
    cpty_count = funding_spread.shape[0]
    bucket_count = risk_weights.shape[0]
    path_rows = basis_values.shape[0]
    owner_of = trade_cpty // cpty_count
    trade_code = trade_cpty % cpty_count * bucket_count + trade_bucket
    position = jnp.arange(per_device, dtype=jnp.int32)
    same_owner = owner_of[:, None] == owner_of[None, :]
    earlier = position[None, :] < position[:, None]
    rank_in = jnp.sum((same_owner & earlier).astype(jnp.int32), axis=1)
    slot_index = owner_of * capacity + rank_in
    codes_out = jnp.full((slot_total,), -1, jnp.int32).at[slot_index].set(trade_code)
    got_codes = lax.all_to_all(codes_out, "trade", split_axis=0, concat_axis=0, tiled=True)
    delta_rows = lax.dot_general(
        basis_values, coefficients, (((1,), (1,)), ((), ())), preferred_element_type=jnp.float32
    ).astype(jnp.bfloat16)
    outgoing = jnp.zeros((path_rows, slot_total), jnp.bfloat16).at[:, slot_index].set(delta_rows)
    arrived = lax.all_to_all(outgoing, "trade", split_axis=1, concat_axis=1, tiled=True)
    margin_now, slot_bar = margin_terms(
        arrived, got_codes, risk_weights, correlation, funding_spread
    )
    returned = lax.all_to_all(slot_bar, "trade", split_axis=1, concat_axis=1, tiled=True)
    delta_bar = returned[:, slot_index]
    partial_adj = jnp.dot(delta_bar, coefficients, preferred_element_type=jnp.float32)
    basis_adjoint = lax.psum(partial_adj, "trade").astype(jnp.bfloat16)
    return (margin_now.T, basis_adjoint)


def solution(mesh):
    placed = (
        P(("date", "path"), None),
        P(("date", "trade"), None),
        P("trade"),
        P("trade"),
        P(),
        P(),
        P("trade"),
    )
    return jax.shard_map(
        body,
        mesh=mesh,
        in_specs=placed,
        out_specs=(P("trade", ("date", "path")), P(("date", "path"), None)),
        check_vma=False,
    )
```

profile of v0, /device:TPU:0, one launch (start us, length us, event | category | flops | bytes accessed | tf_op | source)
XLA Modules:
  0.0 130.3 jit_solution(14144373721821639996)
XLA Ops:
  0.6 0.0 copy-start
  0.6 0.8 fusion.14
  1.4 0.2 convert_reduce_fusion
  1.6 1.1 scatter_custom_fusion.1
  2.7 0.7 all_to_all.25
  3.4 7.3 %all-to-all-start.1 = ((s32[8,40,1]{1,2,0:T(1,128)}), s32[8,40,1]{1,2,0:T(1,128)S(1)}, u32[]{:S(2)}, u32[]{:S(2)}) async-start(s32[8,40,1]{1,2,0:T(1,128)} %all_to_all.25), calls=%async_computation.1 | async-start | bytes 8192 | tf_op jit(solution)/shard_map/all_to_all | solution.py:47
  10.6 0.0 copy-done
  10.7 1.2 fusion.7
  11.9 0.0 copy-start.2
  11.9 0.0 copy-start.3
  11.9 1.9 %scatter_custom_fusion = bf16[512,320]{0,1:T(8,128)(2,1)} fusion(s32[160]{0:T(256)S(1)} %compare_select_fusion.4, bf16[160,512]{1,0:T(8,128)(2,1)S(1)} %fusion.7, bf16[]{:T(256)} %constant.45.clone.1), kind=kCustom, calls=%fused_computation.18 | custom fusion | bytes 327682 | tf_op jit(solution)/shard_map/scatter | solution.py:51
  13.8 3.2 %all-to-all-done.1 = s32[8,40,1]{1,2,0:T(1,128)S(1)} async-done(((s32[8,40,1]{1,2,0:T(1,128)}), s32[8,40,1]{1,2,0:T(1,128)S(1)}, u32[]{:S(2)}, u32[]{:S(2)}) %all-to-all-start.1) | async-done | bytes 1312 | tf_op jit(solution)/shard_map/all_to_all | solution.py:47
  17.0 3.4 %all-to-all-start = ((bf16[512,8,40]{0,2,1:T(8,128)(2,1)}), bf16[512,8,40]{0,2,1:T(8,128)(2,1)S(1)}, u32[]{:S(2)}, u32[]{:S(2)}) async-start(bf16[512,8,40]{0,2,1:T(8,128)(2,1)} %bitcast.1), calls=%async_computation | async-start | bytes 655360 | tf_op jit(solution)/shard_map/all_to_all | solution.py:52
  20.5 0.7 broadcast_multiply_fusion
  21.2 0.5 broadcast.164
  21.7 0.7 reduce.7
  22.4 0.1 eq.51
  22.5 0.1 all_to_all.27
  22.6 6.9 %all-to-all-done = bf16[512,8,40]{0,2,1:T(8,128)(2,1)S(1)} async-done(((bf16[512,8,40]{0,2,1:T(8,128)(2,1)}), bf16[512,8,40]{0,2,1:T(8,128)(2,1)S(1)}, u32[]{:S(2)}, u32[]{:S(2)}) %all-to-all-start) | async-done | bytes 327712 | tf_op jit(solution)/shard_map/all_to_all | solution.py:52
  29.6 1.4 %fusion.2 = f32[512,16,128]{0,2,1:T(8,128)S(1)} fusion(bf16[512,320,1]{0,1,2:T(8,128)(2,1)S(1)} %bitcast.29, s32[16,128]{1,0:T(8,128)S(1)} %multiply_add_fusion, s32[320]{0:T(512)S(1)} %eq.51), kind=kOutput, calls=%fused_computation.8 | convolution fusion | flops 671744000 | bytes 4531456 | tf_op jit(solution)/shard_map/dot_general | solution.py:14
  30.9 0.0 copy-done.2
  31.0 5.5 %multiply_reduce_fusion = (f32[512,16]{0,1:T(8,128)S(1)}, f32[512,16,128]{0,2,1:T(8,128)S(1)}) fusion(f32[512,16,128]{0,2,1:T(8,128)S(1)} %fusion.2, f32[128]{0:T(128)S(1)} %copy-done.3, f32[128,128]{1,0:T(8,128)S(1)} %copy-done.2), kind=kOutput, calls=%fused_computation.5 | convolution fusion | flops 1614798848 | bytes 8487424 | tf_op jit(solution)/shard_map/pcb,db->pcd/dot_general | solution.py:18
  36.4 0.6 add_sqrt_fusion
  37.1 2.4 %multiply_divide_fusion = f32[512,16,128]{0,2,1:T(8,128)} fusion(f32[512,16,128]{0,2,1:T(8,128)S(1)} %get-tuple-element.9, f32[512,16]{0,1:T(8,128)S(1)} %get-tuple-element.2, f32[16,128]{1,0:T(8,128)S(1)} %broadcast_multiply_fusion), kind=kLoop, calls=%fused_computation.4 | loop fusion | flops 2097152 | bytes 8429568 | tf_op jit(solution)/shard_map/div | solution.py:21
  39.5 4.3 %gather_fusion = f32[320,512]{1,0:T(8,128)S(1)} fusion(f32[512,2048]{0,1:T(8,128)} %bitcast.26, s32[1024]{0:T(1024)S(1)} %pad_clamp_fusion.1), kind=kCustom, calls=%fused_computation | custom fusion | bytes 1312000 | tf_op jit(solution)/shard_map/jit(_take)/gather | solution.py:25
  43.8 0.9 multiply_convert_fusion
  44.7 3.6 %all-to-all-start.2 = ((bf16[512,8,40]{0,2,1:T(8,128)(2,1)}), bf16[512,8,40]{0,2,1:T(8,128)(2,1)S(1)}, u32[]{:S(2)}, u32[]{:S(2)}) async-start(bf16[512,8,40]{0,2,1:T(8,128)(2,1)} %multiply_convert_fusion), calls=%async_computation.2 | async-start | bytes 655360 | tf_op jit(solution)/shard_map/all_to_all | solution.py:56
  48.3 9.6 %all-to-all-done.2 = bf16[512,8,40]{0,2,1:T(8,128)(2,1)S(1)} async-done(((bf16[512,8,40]{0,2,1:T(8,128)(2,1)}), bf16[512,8,40]{0,2,1:T(8,128)(2,1)S(1)}, u32[]{:S(2)}, u32[]{:S(2)}) %all-to-all-start.2) | async-done | bytes 327712 | tf_op jit(solution)/shard_map/all_to_all | solution.py:56
  57.9 0.9 gather_fusion.1
  58.8 0.0 copy-done.1
  58.8 0.3 fusion.18
  59.2 71.2 %all-reduce.1 = bf16[512,512]{1,0:T(8,128)(2,1)} all-reduce(f32[512,512]{1,0:T(8,128)S(1)} %fusion.18), channel_id=1, replica_groups=mesh['date'=2,'trade'=8,'path'=2] {'trade'}, use_global_device_ids=true, to_apply=%region_4.5 | all-reduce | flops 262144 | bytes 1572864 | tf_op jit(solution)/shard_map/psum | solution.py:59
  (8 shorter events, 0.1 us)
Async XLA Ops:
  0.6 10.0 %copy-start = (bf16[512,512]{1,0:T(8,128)(2,1)S(1)}, bf16[512,512]{1,0:T(8,128)(2,1)}, u32[]{:S(2)}) copy-start(bf16[512,512]{1,0:T(8,128)(2,1)} %param.7) | copy-start | bytes 1572868
  3.4 13.6 %all-to-all-start.1 = ((s32[8,40,1]{1,2,0:T(1,128)}), s32[8,40,1]{1,2,0:T(1,128)S(1)}, u32[]{:S(2)}, u32[]{:S(2)}) async-start(s32[8,40,1]{1,2,0:T(1,128)} %all_to_all.25), calls=%async_computation.1 | async-start | bytes 8192 | tf_op jit(solution)/shard_map/all_to_all | solution.py:47
  11.9 19.0 %copy-start.2 = (f32[128,128]{1,0:T(8,128)S(1)}, f32[128,128]{1,0:T(8,128)}, u32[]{:S(2)}) copy-start(f32[128,128]{1,0:T(8,128)} %param.12) | copy-start | bytes 196612
  11.9 19.0 %copy-start.3 = (f32[128]{0:T(128)S(1)}, f32[128]{0:T(128)}, u32[]{:S(2)}) copy-start(f32[128]{0:T(128)} %param.11) | copy-start | bytes 1540
  17.0 12.5 %all-to-all-start = ((bf16[512,8,40]{0,2,1:T(8,128)(2,1)}), bf16[512,8,40]{0,2,1:T(8,128)(2,1)S(1)}, u32[]{:S(2)}, u32[]{:S(2)}) async-start(bf16[512,8,40]{0,2,1:T(8,128)(2,1)} %bitcast.1), calls=%async_computation | async-start | bytes 655360 | tf_op jit(solution)/shard_map/all_to_all | solution.py:52
  39.5 19.3 %copy-start.1 = (bf16[160,512]{1,0:T(8,128)(2,1)S(1)}, bf16[160,512]{1,0:T(8,128)(2,1)}, u32[]{:S(2)}) copy-start(bf16[160,512]{1,0:T(8,128)(2,1)} %param.8) | copy-start | bytes 491524
  44.7 13.2 %all-to-all-start.2 = ((bf16[512,8,40]{0,2,1:T(8,128)(2,1)}), bf16[512,8,40]{0,2,1:T(8,128)(2,1)S(1)}, u32[]{:S(2)}, u32[]{:S(2)}) async-start(bf16[512,8,40]{0,2,1:T(8,128)(2,1)} %multiply_convert_fusion), calls=%async_computation.2 | async-start | bytes 655360 | tf_op jit(solution)/shard_map/all_to_all | solution.py:56
where the time goes:
time: 131 us; the launch traced here: 130 us
  blocking collectives  71.2 us (54%)
  waiting for transfers between devices  19.8 us (15%)
  starting transfers between devices  14.3 us (11%)
  local copies, waits for them, and re-layouts  9.56 us (7%)
  matrix products  8.42 us (6%)
  other arithmetic  6.37 us (5%)
    psum x1, blocking collectives, body(): basis_adjoint = lax.psum(partial_adj, 'trade').astype(jnp.bfloat16)  71.2 us
    all_to_all x1, waiting for transfers between devices, body(): lax.all_to_all(slot_bar, 'trade', split_axis=1, concat_axis=1, tiled=True)  9.6 us
    all_to_all x1, starting transfers between devices, body(): lax.all_to_all(codes_out, 'trade', split_axis=0, concat_axis=0, tiled=True)  7.25 us
    all_to_all x1, waiting for transfers between devices, body(): lax.all_to_all(outgoing, 'trade', split_axis=1, concat_axis=1, tiled=True)  6.93 us
    dot_general x1, matrix products, margin_terms(): jnp.einsum('pcb,db->pcd', weighted, correlation, precision=lax.Precision....  5.47 us
    gather x1, local copies, waits for them, and re-layouts, margin_terms(): jnp.take(flat_bar, safe_codes, axis=1)  4.27 us
    all_to_all x1, starting transfers between devices, body(): lax.all_to_all(slot_bar, 'trade', split_axis=1, concat_axis=1, tiled=True)  3.6 us
    all_to_all x1, starting transfers between devices, body(): lax.all_to_all(outgoing, 'trade', split_axis=1, concat_axis=1, tiled=True)  3.43 us
  transfers between devices with their start and end apart: 3, of which 3 were waited for; matrix products, arithmetic and copies ran while one was open for 4% of the time, Pallas kernels for 0%

commit v1 on v0

--- a/solution.py
+++ b/solution.py
@@ -1,7 +1,14 @@
 import jax
 import jax.numpy as jnp
 from jax import lax
+from jax.experimental import pallas as pl
+from jax.experimental.pallas import tpu as pltpu
 from jax.sharding import PartitionSpec as P
+
+F32 = jnp.float32
+BF16 = jnp.bfloat16
+BLOCK = 256
+META_LANES = 256
 
 
 def margin_terms(arrived, got_codes, risk_weights, correlation, funding_spread):
@@ -26,7 +33,7 @@
     return (margin_now, slot_bar.astype(jnp.bfloat16))
 
 
-def body(
+def exchange_body(
     basis_values, coefficients, trade_cpty, trade_bucket, risk_weights, correlation, funding_spread
 ):
     owners = lax.axis_size("trade")
@@ -60,6 +67,157 @@
     return (margin_now.T, basis_adjoint)
 
 
+def dot(a, b):
+    return jnp.dot(a, b, preferred_element_type=F32)
+
+
+def split(x):
+    hi = x.astype(BF16)
+    return hi, (x - hi.astype(F32)).astype(BF16)
+
+
+def one_hot_t(row, count):
+    ids = lax.broadcasted_iota(jnp.int32, (count, row.shape[1]), 0).astype(F32)
+    return (ids == row).astype(F32).astype(BF16)
+
+
+def all_trades_kernel(place_ref, basis_ref, weight_ref, corr_ref, *refs, shards, per, cpties):
+    meta_refs, coef_refs = refs[:shards], refs[shards : 2 * shards]
+    margin_ref, adj_ref = refs[2 * shards : 2 * shards + 2]
+    coef, meta, spread, delta, m_hi, m_lo, r_all, bar, sem = refs[2 * shards + 2 :]
+    trades = shards * per
+    groups = shards * cpties
+    buckets = corr_ref.shape[0]
+    copies = [
+        pltpu.make_async_copy(coef_refs[s], coef.at[pl.ds(s * per, per)], sem.at[s])
+        for s in range(shards)
+    ]
+    for copy in copies:
+        copy.start()
+    for s in range(shards):
+        meta[:, s * per : (s + 1) * per] = meta_refs[s][:, :per]
+        spread[:, s * cpties : (s + 1) * cpties] = meta_refs[s][3:4, :cpties]
+    me, core = place_ref[0], place_ref[1]
+    slot = meta[0:1, :].astype(jnp.int32) ^ me
+    slot = jnp.where(slot >= 2, slot ^ core, slot)
+    group = (slot * cpties).astype(F32) + meta[1:2, :]
+    bucket = meta[2:3, :]
+    group_t = one_hot_t(group, groups)
+    group_hot = group_t.T
+    bucket_t = one_hot_t(bucket, buckets)
+    bucket_hot = bucket_t.T
+    weight = weight_ref[...]
+    weight_col = jnp.broadcast_to(weight, (buckets, buckets)).T
+    c_hi, c_lo = split(corr_ref[...] * weight * weight_col)
+    gathered = jnp.concatenate(
+        [dot(c_hi, bucket_t).astype(BF16), dot(c_lo, bucket_t).astype(BF16)], 0
+    )
+    bucket_two = jnp.concatenate([bucket_hot, bucket_hot], 1)
+    group_col = jnp.broadcast_to(group, (groups, trades)).T[:, :1]
+    blocks = [slice(k, min(k + BLOCK, trades)) for k in range(0, trades, BLOCK)]
+    for cols in blocks:
+        for rows in blocks:
+            pair = dot(bucket_two[rows], gathered[:, cols])
+            pair = jnp.where(group_col[rows] == group[:, cols], pair, 0.0)
+            hi, lo = split(pair)
+            m_hi[rows, cols] = hi
+            m_lo[rows, cols] = lo
+    for copy in copies:
+        copy.wait()
+    for cols in blocks:
+        delta[:, cols] = lax.dot_general(
+            basis_ref[...], coef[cols, :], (((1,), (1,)), ((), ())), preferred_element_type=F32
+        ).astype(BF16)
+    squares = None
+    for cols in blocks:
+        r = dot(delta[...], m_hi[:, cols]) + dot(delta[...], m_lo[:, cols])
+        r_all[:, cols] = r
+        hi, lo = split(delta[:, cols].astype(F32) * r)
+        part = dot(hi, group_hot[cols]) + dot(lo, group_hot[cols])
+        squares = part if squares is None else squares + part
+    margin = jnp.sqrt(squares + 1e-06)
+    margin_ref[...] = margin.T[:cpties]
+    hi, lo = split(spread[...] / margin)
+    scale = jnp.concatenate([hi, lo], 1)
+    group_two = jnp.concatenate([group_t, group_t], 0)
+    for cols in blocks:
+        bar[:, cols] = (r_all[:, cols] * dot(scale, group_two[:, cols])).astype(BF16)
+    adj_ref[...] = dot(bar[...], coef[...]).astype(BF16)
+
+
+def swap_cores(x):
+    return lax.ppermute(x, "path", [(0, 1), (1, 0)])
+
+
+def fetch(x, first, second, owners):
+    pairs = [(i * 2, (i ^ first) * 2) for i in range(owners)]
+    pairs += [(i * 2 + 1, (i ^ second) * 2 + 1) for i in range(owners)]
+    return lax.ppermute(x, ("trade", "path"), pairs)
+
+
+def gather_shards(x, owners):
+    far = fetch(x, 4, 5, owners)
+    farther = fetch(x, 6, 7, owners)
+    near = fetch(x, 2, 3, owners)
+    beside = fetch(x, 1, 1, owners)
+    return [x, beside, near, swap_cores(near), far, swap_cores(far), farther, swap_cores(farther)]
+
+
+def gather_body(
+    basis_values, coefficients, trade_cpty, trade_bucket, risk_weights, correlation, funding_spread
+):
+    owners = lax.axis_size("trade")
+    per = coefficients.shape[0]
+    cpties = funding_spread.shape[0]
+    buckets = risk_weights.shape[0]
+    paths, width = basis_values.shape
+    trades = owners * per
+
+    def row(x):
+        return jnp.pad(x.astype(F32), (0, META_LANES - x.shape[0]))
+
+    meta = jnp.stack(
+        [
+            row(trade_cpty // cpties),
+            row(trade_cpty % cpties),
+            row(trade_bucket),
+            row(funding_spread),
+        ]
+    )
+    meta = jnp.pad(meta, ((0, 4), (0, 0)))
+    coef_all = gather_shards(coefficients, owners)
+    meta_all = gather_shards(meta, owners)
+    place = jnp.stack([lax.axis_index("trade"), lax.axis_index("path")]).astype(jnp.int32)
+    vmem = pl.BlockSpec(memory_space=pltpu.VMEM)
+
+    def kernel(*refs):
+        all_trades_kernel(*refs, shards=owners, per=per, cpties=cpties)
+
+    return pl.pallas_call(
+        kernel,
+        out_shape=[
+            jax.ShapeDtypeStruct((cpties, paths), F32),
+            jax.ShapeDtypeStruct((paths, width), BF16),
+        ],
+        in_specs=[pl.BlockSpec(memory_space=pltpu.SMEM)]
+        + [vmem] * (3 + owners)
+        + [pl.BlockSpec(memory_space=pl.ANY)] * owners,
+        out_specs=[vmem, vmem],
+        scratch_shapes=[
+            pltpu.VMEM((trades, width), BF16),
+            pltpu.VMEM((8, trades), F32),
+            pltpu.VMEM((1, owners * cpties), F32),
+            pltpu.VMEM((paths, trades), BF16),
+            pltpu.VMEM((trades, trades), BF16),
+            pltpu.VMEM((trades, trades), BF16),
+            pltpu.VMEM((paths, trades), F32),
+            pltpu.VMEM((paths, trades), BF16),
+            pltpu.SemaphoreType.DMA((owners,)),
+        ],
+        compiler_params=pltpu.CompilerParams(vmem_limit_bytes=56 << 20),
+    )(place, basis_values, risk_weights.reshape(1, buckets), correlation, *meta_all, *coef_all)
+
+
 def solution(mesh):
     placed = (
         P(("date", "path"), None),
@@ -70,8 +228,9 @@
         P(),
         P("trade"),
     )
+    small = mesh.shape["trade"] == 8 and mesh.shape["path"] == 2
     return jax.shard_map(
-        body,
+        gather_body if small else exchange_body,
         mesh=mesh,
         in_specs=placed,
         out_specs=(P("trade", ("date", "path")), P(("date", "path"), None)),

time: 131 us -> 54.3 us (0.41)
  blocking collectives: 71.2 us -> 0 us
  Pallas kernels: 0 us -> 13.8 us
  matrix products: 8.42 us -> 0 us
  local copies, waits for them, and re-layouts: 9.56 us -> 2.08 us
  other arithmetic: 6.37 us -> 1.37 us
  starting transfers between devices: 14.3 us -> 16.6 us
    psum x1 -> x0, blocking collectives: 71.2 us -> none  [body(): basis_adjoint = lax.psum(partial_adj, 'trade').astype(jnp.bfloat16)]
    all_to_all x3 -> x0, waiting for transfers between devices: 19.8 us -> none  [the longest x1 9.6 us: body(): lax.all_to_all(slot_bar, 'trade', split_axis=1, concat_axis=1, tiled=True)]
    ppermute x0 -> x14, waiting for transfers between devices: none -> 19.5 us  [the longest x8 16.9 us: fetch(): return lax.ppermute(x, ('trade', 'path'), pairs)]
    ppermute x0 -> x14, starting transfers between devices: none -> 16.6 us  [the longest x8 15.8 us: fetch(): return lax.ppermute(x, ('trade', 'path'), pairs)]
    all_to_all x3 -> x0, starting transfers between devices: 14.3 us -> none  [the longest x1 7.25 us: body(): lax.all_to_all(codes_out, 'trade', split_axis=0, concat_axis=0, tiled=True)]
    pallas_call x0 -> x1, Pallas kernels: none -> 13.8 us  [gather_body(): pl.pallas_call(kernel, out_shape=[jax.ShapeDtypeStruct((cpties, paths), F...]
    dot_general x4 -> x0, matrix products: 8.42 us -> none  [the longest x1 5.47 us: margin_terms(): jnp.einsum('pcb,db->pcd', weighted, correlation, precision=lax.Precision....]
    gather x2 -> x0, local copies, waits for them, and re-layouts: 5.2 us -> none  [the longest x1 4.27 us: margin_terms(): jnp.take(flat_bar, safe_codes, axis=1)]
  transfers between devices with their start and end apart: 3 -> 14, of which waited for: 3 -> 10; matrix products, arithmetic and copies ran while one was open for 4% -> 3% of each run, Pallas kernels for 0% -> 0%
where the time goes in v1:
time: 54.3 us; the launch traced here: 54.1 us
  waiting for transfers between devices  19.5 us (36%)
  starting transfers between devices  16.6 us (31%)
  Pallas kernels  13.8 us (25%)
  local copies, waits for them, and re-layouts  2.08 us (4%)
  other arithmetic  1.37 us (3%)
  between operations  0.79 us (1%)
    ppermute x8, waiting for transfers between devices, fetch(): return lax.ppermute(x, ('trade', 'path'), pairs)  16.9 us
    ppermute x8, starting transfers between devices, fetch(): return lax.ppermute(x, ('trade', 'path'), pairs)  15.8 us
    pallas_call x1, Pallas kernels, gather_body(): pl.pallas_call(kernel, out_shape=[jax.ShapeDtypeStruct((cpties, paths), F...  13.8 us
    ppermute x6, waiting for transfers between devices, swap_cores(): return lax.ppermute(x, 'path', [(0, 1), (1, 0)])  2.52 us
    unnamed x34, local copies, waits for them, and re-layouts  2.07 us
  transfers between devices with their start and end apart: 14, of which 10 were waited for; matrix products, arithmetic and copies ran while one was open for 3% of the time, Pallas kernels for 0%

profile of v1, /device:TPU:0, one launch (start us, length us, event | category | flops | bytes accessed | tf_op | source)
XLA Modules:
  0.0 54.1 jit_solution(18160890014348979926)
XLA Ops:
  0.6 4.1 %collective-permute-start.10 = (bf16[160,512]{1,0:T(8,128)(2,1)}, bf16[160,512]{1,0:T(8,128)(2,1)S(1)}, u32[]{:S(2)}, u32[]{:S(2)}) collective-permute-start(bf16[160,512]{1,0:T(8,128)(2,1)} %refs_12_.1), channel_id=1, source_target_pairs={{0,8},{2,10},{4,12},{6,14},{8,0},{10,2},{12,4},{14,6},{1,11},{3,9}... | collective-permute-start | bytes 491528 | tf_op jit(solution)/shard_map/ppermute | solution.py:155
  4.7 1.6 %collective-permute-start.8 = (bf16[160,512]{1,0:T(8,128)(2,1)}, bf16[160,512]{1,0:T(8,128)(2,1)S(1)}, u32[]{:S(2)}, u32[]{:S(2)}) collective-permute-start(bf16[160,512]{1,0:T(8,128)(2,1)} %refs_12_.1), channel_id=1, source_target_pairs={{0,4},{2,6},{4,0},{6,2},{8,12},{10,14},{12,8},{14,10},{1,7},{3,5},... | collective-permute-start | bytes 491528 | tf_op jit(solution)/shard_map/ppermute | solution.py:155
  6.3 1.5 %collective-permute-start.7 = (bf16[160,512]{1,0:T(8,128)(2,1)}, bf16[160,512]{1,0:T(8,128)(2,1)S(1)}, u32[]{:S(2)}, u32[]{:S(2)}) collective-permute-start(bf16[160,512]{1,0:T(8,128)(2,1)} %refs_12_.1), channel_id=1, source_target_pairs={{0,2},{2,0},{4,6},{6,4},{8,10},{10,8},{12,14},{14,12},{1,3},{3,1},... | collective-permute-start | bytes 491528 | tf_op jit(solution)/shard_map/ppermute | solution.py:155
  7.8 0.2 collective-permute-start.12
  8.0 0.7 %convert_element_type.19 = f32[160]{0:T(256)S(1)} convert(s32[160]{0:T(256)} %param.10) | non-fusion elementwise | flops 160 | bytes 1280 | tf_op jit(solution)/shard_map/convert_element_type | solution.py:177
  8.7 0.6 %copy-done.16 = f32[16]{0:T(128)S(1)} copy-done((f32[16]{0:T(128)S(1)}, f32[16]{0:T(128)}, u32[]{:S(2)}) %copy-start.16) | copy-done | bytes 88
  9.4 0.7 %copy-done.15 = s32[160]{0:T(256)S(1)} copy-done((s32[160]{0:T(256)S(1)}, s32[160]{0:T(256)}, u32[]{:S(2)}) %copy-start.15) | copy-done | bytes 664
  10.1 3.4 %collective-permute-done.10.refs_16_ = bf16[160,512]{1,0:T(8,128)(2,1)S(1)} collective-permute-done((bf16[160,512]{1,0:T(8,128)(2,1)}, bf16[160,512]{1,0:T(8,128)(2,1)S(1)}, u32[]{:S(2)}, u32[]{:S(2)}) %collective-permute-start.10) | collective-permute-done | bytes 163872 | tf_op jit(solution)/shard_map/ppermute | solution.py:155
  13.5 0.3 collective-permute-done.8.refs_14_
  13.8 0.4 collective-permute-start.9
  14.2 4.1 %collective-permute-done.12.refs_18_ = bf16[160,512]{1,0:T(8,128)(2,1)S(1)} collective-permute-done((bf16[160,512]{1,0:T(8,128)(2,1)}, bf16[160,512]{1,0:T(8,128)(2,1)S(1)}, u32[]{:S(2)}, u32[]{:S(2)}) %collective-permute-start.12) | collective-permute-done | bytes 163872 | tf_op jit(solution)/shard_map/ppermute | solution.py:155
  18.3 0.0 collective-permute-start.13
  18.3 2.5 %collective-permute-start.5 = (f32[8,256]{1,0:T(8,128)S(1)}, f32[8,256]{1,0:T(8,128)S(1)}, u32[]{:S(2)}, u32[]{:S(2)}) collective-permute-start(f32[8,256]{1,0:T(8,128)S(1)} %select_maximum_fusion.refs_4_), channel_id=1, source_target_pairs={{0,12},{2,14},{4,8},{6,10},{8,4},{10,6},{12,0},{14,2},{1,15},{3,13... | collective-permute-start | bytes 24584 | tf_op jit(solution)/shard_map/ppermute | solution.py:155
  20.9 3.0 %collective-permute-done.5.refs_10_ = f32[8,256]{1,0:T(8,128)S(1)} collective-permute-done((f32[8,256]{1,0:T(8,128)S(1)}, f32[8,256]{1,0:T(8,128)S(1)}, u32[]{:S(2)}, u32[]{:S(2)}) %collective-permute-start.5) | collective-permute-done | bytes 8224 | tf_op jit(solution)/shard_map/ppermute | solution.py:155
  23.8 3.1 %collective-permute-start.3 = (f32[8,256]{1,0:T(8,128)S(1)}, f32[8,256]{1,0:T(8,128)S(1)}, u32[]{:S(2)}, u32[]{:S(2)}) collective-permute-start(f32[8,256]{1,0:T(8,128)S(1)} %select_maximum_fusion.refs_4_), channel_id=1, source_target_pairs={{0,8},{2,10},{4,12},{6,14},{8,0},{10,2},{12,4},{14,6},{1,11},{3,9}... | collective-permute-start | bytes 24584 | tf_op jit(solution)/shard_map/ppermute | solution.py:155
  27.0 1.6 %collective-permute-done.3.refs_8_ = f32[8,256]{1,0:T(8,128)S(1)} collective-permute-done((f32[8,256]{1,0:T(8,128)S(1)}, f32[8,256]{1,0:T(8,128)S(1)}, u32[]{:S(2)}, u32[]{:S(2)}) %collective-permute-start.3) | collective-permute-done | bytes 8224 | tf_op jit(solution)/shard_map/ppermute | solution.py:155
  28.6 1.5 %collective-permute-start.1 = (f32[8,256]{1,0:T(8,128)S(1)}, f32[8,256]{1,0:T(8,128)S(1)}, u32[]{:S(2)}, u32[]{:S(2)}) collective-permute-start(f32[8,256]{1,0:T(8,128)S(1)} %select_maximum_fusion.refs_4_), channel_id=1, source_target_pairs={{0,4},{2,6},{4,0},{6,2},{8,12},{10,14},{12,8},{14,10},{1,7},{3,5},... | collective-permute-start | bytes 24584 | tf_op jit(solution)/shard_map/ppermute | solution.py:155
  30.1 2.2 %collective-permute-done.1.refs_6_ = f32[8,256]{1,0:T(8,128)S(1)} collective-permute-done((f32[8,256]{1,0:T(8,128)S(1)}, f32[8,256]{1,0:T(8,128)S(1)}, u32[]{:S(2)}, u32[]{:S(2)}) %collective-permute-start.1) | collective-permute-done | bytes 8224 | tf_op jit(solution)/shard_map/ppermute | solution.py:155
  32.3 1.3 %collective-permute-start = (f32[8,256]{1,0:T(8,128)S(1)}, f32[8,256]{1,0:T(8,128)S(1)}, u32[]{:S(2)}, u32[]{:S(2)}) collective-permute-start(f32[8,256]{1,0:T(8,128)S(1)} %select_maximum_fusion.refs_4_), channel_id=1, source_target_pairs={{0,2},{2,0},{4,6},{6,4},{8,10},{10,8},{12,14},{14,12},{1,3},{3,1},... | collective-permute-start | bytes 24584 | tf_op jit(solution)/shard_map/ppermute | solution.py:155
  33.5 2.4 %collective-permute-done.refs_5_ = f32[8,256]{1,0:T(8,128)S(1)} collective-permute-done((f32[8,256]{1,0:T(8,128)S(1)}, f32[8,256]{1,0:T(8,128)S(1)}, u32[]{:S(2)}, u32[]{:S(2)}) %collective-permute-start) | collective-permute-done | bytes 8224 | tf_op jit(solution)/shard_map/ppermute | solution.py:155
  35.9 1.2 %collective-permute-done.6.refs_11_ = f32[8,256]{1,0:T(8,128)S(1)} collective-permute-done((f32[8,256]{1,0:T(8,128)S(1)}, f32[8,256]{1,0:T(8,128)S(1)}, u32[]{:S(2)}, u32[]{:S(2)}) %collective-permute-start.6) | collective-permute-done | bytes 8224 | tf_op jit(solution)/shard_map/ppermute | solution.py:149
  37.1 0.2 collective-permute-start.4
  37.3 1.0 %collective-permute-done.4.refs_9_ = f32[8,256]{1,0:T(8,128)S(1)} collective-permute-done((f32[8,256]{1,0:T(8,128)S(1)}, f32[8,256]{1,0:T(8,128)S(1)}, u32[]{:S(2)}, u32[]{:S(2)}) %collective-permute-start.4) | collective-permute-done | bytes 8224 | tf_op jit(solution)/shard_map/ppermute | solution.py:149
  38.3 0.2 collective-permute-start.2
  38.4 0.7 %pad_add_fusion.refs_0_ = s32[2]{0:T(128)} fusion(s32[1]{0:T(128)} %bitcast.1, s32[1]{0:T(128)} %bitcast), kind=kLoop, calls=%fused_computation.11 | loop fusion | flops 2 | bytes 16 | tf_op jit(solution)/shard_map/stack | solution.py:190
  39.1 0.3 collective-permute-done.2.refs_7_
  39.6 0.5 copy-done.14
  40.0 0.1 copy-done.2
  40.1 0.1 copy-done.4
  40.2 0.0 copy-done.5
  40.3 0.0 copy-done.6
  40.3 13.8 %shard_map.86 = (f32[16,512]{1,0:T(8,128)}, bf16[512,512]{1,0:T(8,128)(2,1)}) custom-call(s32[2]{0:T(128)} %pad_add_fusion.refs_0_, bf16[512,512]{1,0:T(8,128)(2,1)} %refs_1_.1, f32[1,128]{1,0:T(1,128)} %bitcast.11, f32[128,128]{1,0:T(8,128)} %refs_3_.1, f32[8,256]{1,0:T(8,128)} %copy-done.7, f32[8,256]{1,0:T(8,128)} %copy-done.11, f32[8,256]{1,0:T(8,128)} %copy-done.10, ...), custom_call_target="tpu_custom_call" | custom-call | tf_op jit(solution)/shard_map/pallas_call | solution.py:196
  (39 shorter events, 0.1 us)
Async XLA Ops:
  0.6 12.9 %collective-permute-start.10 = (bf16[160,512]{1,0:T(8,128)(2,1)}, bf16[160,512]{1,0:T(8,128)(2,1)S(1)}, u32[]{:S(2)}, u32[]{:S(2)}) collective-permute-start(bf16[160,512]{1,0:T(8,128)(2,1)} %refs_12_.1), channel_id=1, source_target_pairs={{0,8},{2,10},{4,12},{6,14},{8,0},{10,2},{12,4},{14,6},{1,11},{3,9}... | collective-permute-start | bytes 491528 | tf_op jit(solution)/shard_map/ppermute | solution.py:155
  4.7 9.0 %collective-permute-start.8 = (bf16[160,512]{1,0:T(8,128)(2,1)}, bf16[160,512]{1,0:T(8,128)(2,1)S(1)}, u32[]{:S(2)}, u32[]{:S(2)}) collective-permute-start(bf16[160,512]{1,0:T(8,128)(2,1)} %refs_12_.1), channel_id=1, source_target_pairs={{0,4},{2,6},{4,0},{6,2},{8,12},{10,14},{12,8},{14,10},{1,7},{3,5},... | collective-permute-start | bytes 491528 | tf_op jit(solution)/shard_map/ppermute | solution.py:155
  6.3 33.1 %collective-permute-start.7 = (bf16[160,512]{1,0:T(8,128)(2,1)}, bf16[160,512]{1,0:T(8,128)(2,1)S(1)}, u32[]{:S(2)}, u32[]{:S(2)}) collective-permute-start(bf16[160,512]{1,0:T(8,128)(2,1)} %refs_12_.1), channel_id=1, source_target_pairs={{0,2},{2,0},{4,6},{6,4},{8,10},{10,8},{12,14},{14,12},{1,3},{3,1},... | collective-permute-start | bytes 491528 | tf_op jit(solution)/shard_map/ppermute | solution.py:155
  7.8 10.5 %collective-permute-start.12 = (bf16[160,512]{1,0:T(8,128)(2,1)}, bf16[160,512]{1,0:T(8,128)(2,1)S(1)}, u32[]{:S(2)}, u32[]{:S(2)}) collective-permute-start(bf16[160,512]{1,0:T(8,128)(2,1)} %refs_12_.1), channel_id=1, source_target_pairs={{0,12},{2,14},{4,8},{6,10},{8,4},{10,6},{12,0},{14,2},{1,15},{3,13... | collective-permute-start | bytes 491528 | tf_op jit(solution)/shard_map/ppermute | solution.py:155
  8.7 0.7 %copy-start.16 = (f32[16]{0:T(128)S(1)}, f32[16]{0:T(128)}, u32[]{:S(2)}) copy-start(f32[16]{0:T(128)} %param.13) | copy-start | bytes 196
  9.4 0.7 %copy-start.15 = (s32[160]{0:T(256)S(1)}, s32[160]{0:T(256)}, u32[]{:S(2)}) copy-start(s32[160]{0:T(256)} %param.9) | copy-start | bytes 1924
  13.5 26.0 %copy-start = (bf16[160,512]{1,0:T(8,128)(2,1)}, bf16[160,512]{1,0:T(8,128)(2,1)S(1)}, u32[]{:S(2)}) copy-start(bf16[160,512]{1,0:T(8,128)(2,1)S(1)} %collective-permute-done.10.refs_16_) | copy-start | bytes 491524
  13.5 26.0 %collective-permute-start.11 = (bf16[160,512]{1,0:T(8,128)(2,1)S(1)}, bf16[160,512]{1,0:T(8,128)(2,1)S(1)}, u32[]{:S(2)}, u32[]{:S(2)}) collective-permute-start(bf16[160,512]{1,0:T(8,128)(2,1)S(1)} %collective-permute-done.10.refs_16_), channel_id=1, source_target_pairs={{0,1},{1,0},{2,3},{3,2},{4,5},{5,4},{6,7},{7,6},{8,9},{9,8},{10,11... | collective-permute-start | bytes 491528 | tf_op jit(solution)/shard_map/ppermute | solution.py:149
  13.8 25.8 %copy-start.1 = (bf16[160,512]{1,0:T(8,128)(2,1)}, bf16[160,512]{1,0:T(8,128)(2,1)S(1)}, u32[]{:S(2)}) copy-start(bf16[160,512]{1,0:T(8,128)(2,1)S(1)} %collective-permute-done.8.refs_14_) | copy-start | bytes 491524
  13.8 25.7 %collective-permute-start.9 = (bf16[160,512]{1,0:T(8,128)(2,1)S(1)}, bf16[160,512]{1,0:T(8,128)(2,1)S(1)}, u32[]{:S(2)}, u32[]{:S(2)}) collective-permute-start(bf16[160,512]{1,0:T(8,128)(2,1)S(1)} %collective-permute-done.8.refs_14_), channel_id=1, source_target_pairs={{0,1},{1,0},{2,3},{3,2},{4,5},{5,4},{6,7},{7,6},{8,9},{9,8},{10,11... | collective-permute-start | bytes 491528 | tf_op jit(solution)/shard_map/ppermute | solution.py:149
  18.3 21.2 %copy-start.3 = (bf16[160,512]{1,0:T(8,128)(2,1)}, bf16[160,512]{1,0:T(8,128)(2,1)S(1)}, u32[]{:S(2)}) copy-start(bf16[160,512]{1,0:T(8,128)(2,1)S(1)} %collective-permute-done.12.refs_18_) | copy-start | bytes 491524
  18.3 21.2 %collective-permute-start.13 = (bf16[160,512]{1,0:T(8,128)(2,1)S(1)}, bf16[160,512]{1,0:T(8,128)(2,1)S(1)}, u32[]{:S(2)}, u32[]{:S(2)}) collective-permute-start(bf16[160,512]{1,0:T(8,128)(2,1)S(1)} %collective-permute-done.12.refs_18_), channel_id=1, source_target_pairs={{0,1},{1,0},{2,3},{3,2},{4,5},{5,4},{6,7},{7,6},{8,9},{9,8},{10,11... | collective-permute-start | bytes 491528 | tf_op jit(solution)/shard_map/ppermute | solution.py:149
  18.3 20.8 %copy-start.7 = (f32[8,256]{1,0:T(8,128)}, f32[8,256]{1,0:T(8,128)S(1)}, u32[]{:S(2)}) copy-start(f32[8,256]{1,0:T(8,128)S(1)} %select_maximum_fusion.refs_4_) | copy-start | bytes 24580
  18.3 5.5 %collective-permute-start.5 = (f32[8,256]{1,0:T(8,128)S(1)}, f32[8,256]{1,0:T(8,128)S(1)}, u32[]{:S(2)}, u32[]{:S(2)}) collective-permute-start(f32[8,256]{1,0:T(8,128)S(1)} %select_maximum_fusion.refs_4_), channel_id=1, source_target_pairs={{0,12},{2,14},{4,8},{6,10},{8,4},{10,6},{12,0},{14,2},{1,15},{3,13... | collective-permute-start | bytes 24584 | tf_op jit(solution)/shard_map/ppermute | solution.py:155
  23.8 15.3 %copy-start.8 = (f32[8,256]{1,0:T(8,128)}, f32[8,256]{1,0:T(8,128)S(1)}, u32[]{:S(2)}) copy-start(f32[8,256]{1,0:T(8,128)S(1)} %collective-permute-done.5.refs_10_) | copy-start | bytes 24580
  23.8 4.8 %collective-permute-start.3 = (f32[8,256]{1,0:T(8,128)S(1)}, f32[8,256]{1,0:T(8,128)S(1)}, u32[]{:S(2)}, u32[]{:S(2)}) collective-permute-start(f32[8,256]{1,0:T(8,128)S(1)} %select_maximum_fusion.refs_4_), channel_id=1, source_target_pairs={{0,8},{2,10},{4,12},{6,14},{8,0},{10,2},{12,4},{14,6},{1,11},{3,9}... | collective-permute-start | bytes 24584 | tf_op jit(solution)/shard_map/ppermute | solution.py:155
  28.6 10.9 %copy-start.9 = (f32[8,256]{1,0:T(8,128)}, f32[8,256]{1,0:T(8,128)S(1)}, u32[]{:S(2)}) copy-start(f32[8,256]{1,0:T(8,128)S(1)} %collective-permute-done.3.refs_8_) | copy-start | bytes 24580
  28.6 3.7 %collective-permute-start.1 = (f32[8,256]{1,0:T(8,128)S(1)}, f32[8,256]{1,0:T(8,128)S(1)}, u32[]{:S(2)}, u32[]{:S(2)}) collective-permute-start(f32[8,256]{1,0:T(8,128)S(1)} %select_maximum_fusion.refs_4_), channel_id=1, source_target_pairs={{0,4},{2,6},{4,0},{6,2},{8,12},{10,14},{12,8},{14,10},{1,7},{3,5},... | collective-permute-start | bytes 24584 | tf_op jit(solution)/shard_map/ppermute | solution.py:155
  32.3 7.3 %copy-start.10 = (f32[8,256]{1,0:T(8,128)}, f32[8,256]{1,0:T(8,128)S(1)}, u32[]{:S(2)}) copy-start(f32[8,256]{1,0:T(8,128)S(1)} %collective-permute-done.1.refs_6_) | copy-start | bytes 24580
  32.3 3.7 %collective-permute-start = (f32[8,256]{1,0:T(8,128)S(1)}, f32[8,256]{1,0:T(8,128)S(1)}, u32[]{:S(2)}, u32[]{:S(2)}) collective-permute-start(f32[8,256]{1,0:T(8,128)S(1)} %select_maximum_fusion.refs_4_), channel_id=1, source_target_pairs={{0,2},{2,0},{4,6},{6,4},{8,10},{10,8},{12,14},{14,12},{1,3},{3,1},... | collective-permute-start | bytes 24584 | tf_op jit(solution)/shard_map/ppermute | solution.py:155
  35.9 3.6 %copy-start.11 = (f32[8,256]{1,0:T(8,128)}, f32[8,256]{1,0:T(8,128)S(1)}, u32[]{:S(2)}) copy-start(f32[8,256]{1,0:T(8,128)S(1)} %collective-permute-done.refs_5_) | copy-start | bytes 24580
  35.9 1.2 %collective-permute-start.6 = (f32[8,256]{1,0:T(8,128)S(1)}, f32[8,256]{1,0:T(8,128)S(1)}, u32[]{:S(2)}, u32[]{:S(2)}) collective-permute-start(f32[8,256]{1,0:T(8,128)S(1)} %collective-permute-done.5.refs_10_), channel_id=1, source_target_pairs={{0,1},{1,0},{2,3},{3,2},{4,5},{5,4},{6,7},{7,6},{8,9},{9,8},{10,11... | collective-permute-start | bytes 24584 | tf_op jit(solution)/shard_map/ppermute | solution.py:149
  37.1 2.5 %copy-start.12 = (f32[8,256]{1,0:T(8,128)}, f32[8,256]{1,0:T(8,128)S(1)}, u32[]{:S(2)}) copy-start(f32[8,256]{1,0:T(8,128)S(1)} %collective-permute-done.6.refs_11_) | copy-start | bytes 24580
  37.1 1.2 %collective-permute-start.4 = (f32[8,256]{1,0:T(8,128)S(1)}, f32[8,256]{1,0:T(8,128)S(1)}, u32[]{:S(2)}, u32[]{:S(2)}) collective-permute-start(f32[8,256]{1,0:T(8,128)S(1)} %collective-permute-done.3.refs_8_), channel_id=1, source_target_pairs={{0,1},{1,0},{2,3},{3,2},{4,5},{5,4},{6,7},{7,6},{8,9},{9,8},{10,11... | collective-permute-start | bytes 24584 | tf_op jit(solution)/shard_map/ppermute | solution.py:149
  38.3 1.3 %copy-start.13 = (f32[8,256]{1,0:T(8,128)}, f32[8,256]{1,0:T(8,128)S(1)}, u32[]{:S(2)}) copy-start(f32[8,256]{1,0:T(8,128)S(1)} %collective-permute-done.4.refs_9_) | copy-start | bytes 24580
  38.3 1.2 %collective-permute-start.2 = (f32[8,256]{1,0:T(8,128)S(1)}, f32[8,256]{1,0:T(8,128)S(1)}, u32[]{:S(2)}, u32[]{:S(2)}) collective-permute-start(f32[8,256]{1,0:T(8,128)S(1)} %collective-permute-done.1.refs_6_), channel_id=1, source_target_pairs={{0,1},{1,0},{2,3},{3,2},{4,5},{5,4},{6,7},{7,6},{8,9},{9,8},{10,11... | collective-permute-start | bytes 24584 | tf_op jit(solution)/shard_map/ppermute | solution.py:149
  39.5 0.6 %copy-start.14 = (f32[8,256]{1,0:T(8,128)}, f32[8,256]{1,0:T(8,128)S(1)}, u32[]{:S(2)}) copy-start(f32[8,256]{1,0:T(8,128)S(1)} %collective-permute-done.2.refs_7_) | copy-start | bytes 24580
  39.5 0.7 %copy-start.2 = (bf16[160,512]{1,0:T(8,128)(2,1)}, bf16[160,512]{1,0:T(8,128)(2,1)S(1)}, u32[]{:S(2)}) copy-start(bf16[160,512]{1,0:T(8,128)(2,1)S(1)} %collective-permute-done.7.refs_13_) | copy-start | bytes 491524
  39.5 0.8 %copy-start.4 = (bf16[160,512]{1,0:T(8,128)(2,1)}, bf16[160,512]{1,0:T(8,128)(2,1)S(1)}, u32[]{:S(2)}) copy-start(bf16[160,512]{1,0:T(8,128)(2,1)S(1)} %collective-permute-done.11.refs_17_) | copy-start | bytes 491524
  39.5 0.8 %copy-start.5 = (bf16[160,512]{1,0:T(8,128)(2,1)}, bf16[160,512]{1,0:T(8,128)(2,1)S(1)}, u32[]{:S(2)}) copy-start(bf16[160,512]{1,0:T(8,128)(2,1)S(1)} %collective-permute-done.9.refs_15_) | copy-start | bytes 491524
  39.5 0.8 %copy-start.6 = (bf16[160,512]{1,0:T(8,128)(2,1)}, bf16[160,512]{1,0:T(8,128)(2,1)S(1)}, u32[]{:S(2)}) copy-start(bf16[160,512]{1,0:T(8,128)(2,1)S(1)} %collective-permute-done.13.refs_19_) | copy-start | bytes 491524

commit v2 on v1

--- a/solution.py
+++ b/solution.py
@@ -8,7 +8,7 @@
 F32 = jnp.float32
 BF16 = jnp.bfloat16
 BLOCK = 256
-META_LANES = 256
+META_ROWS = 8
 
 
 def margin_terms(arrived, got_codes, risk_weights, correlation, funding_spread):
@@ -81,22 +81,63 @@
     return (ids == row).astype(F32).astype(BF16)
 
 
+def pack_kernel(cpty_ref, bucket_ref, spread_ref, coef_ref, out_ref, meta, sem, *, cpties):
+    per, width = coef_ref.shape
+    body = pltpu.make_async_copy(coef_ref, out_ref.at[pl.ds(0, per)], sem.at[0])
+    body.start()
+    cpty = cpty_ref[...]
+    owner = cpty // cpties
+    meta[...] = jnp.zeros_like(meta)
+    meta[0:1, :per] = owner.astype(F32)
+    meta[1:2, :per] = (cpty - owner * cpties).astype(F32)
+    meta[2:3, :per] = bucket_ref[...].astype(F32)
+    spread = spread_ref[...]
+    high = spread.astype(BF16).astype(F32)
+    middle = (spread - high).astype(BF16).astype(F32)
+    meta[3:4, :cpties] = high
+    meta[4:5, :cpties] = middle
+    meta[5:6, :cpties] = spread - high - middle
+    rows = meta.shape[0]
+
+    def tail(block):
+        block[...] = meta[...].astype(BF16)
+        copy = pltpu.make_async_copy(block, out_ref.at[pl.ds(per, rows)], sem.at[1])
+        copy.start()
+        copy.wait()
+
+    pl.run_scoped(tail, pltpu.VMEM((rows, width), BF16))
+    body.wait()
+
+
 def all_trades_kernel(place_ref, basis_ref, weight_ref, corr_ref, *refs, shards, per, cpties):
-    meta_refs, coef_refs = refs[:shards], refs[shards : 2 * shards]
-    margin_ref, adj_ref = refs[2 * shards : 2 * shards + 2]
-    coef, meta, spread, delta, m_hi, m_lo, r_all, bar, sem = refs[2 * shards + 2 :]
+    shard_refs = refs[:shards]
+    margin_ref, adj_ref = refs[shards : shards + 2]
+    coef, tails, meta, spread, delta, m_hi, m_lo, r_all, bar, sem = refs[shards + 2 :]
     trades = shards * per
     groups = shards * cpties
     buckets = corr_ref.shape[0]
-    copies = [
-        pltpu.make_async_copy(coef_refs[s], coef.at[pl.ds(s * per, per)], sem.at[s])
+    heads = [
+        pltpu.make_async_copy(
+            shard_refs[s].at[pl.ds(per, META_ROWS)], tails.at[pl.ds(s * META_ROWS, META_ROWS)], sem.at[s]
+        )
         for s in range(shards)
     ]
-    for copy in copies:
+    copies = [
+        pltpu.make_async_copy(
+            shard_refs[s].at[pl.ds(0, per)], coef.at[pl.ds(s * per, per)], sem.at[shards + s]
+        )
+        for s in range(shards)
+    ]
+    for copy in heads + copies:
         copy.start()
+    for copy in heads:
+        copy.wait()
     for s in range(shards):
-        meta[:, s * per : (s + 1) * per] = meta_refs[s][:, :per]
-        spread[:, s * cpties : (s + 1) * cpties] = meta_refs[s][3:4, :cpties]
+        tail = tails[s * META_ROWS : (s + 1) * META_ROWS, :].astype(F32)
+        meta[:, s * per : (s + 1) * per] = tail[:, :per]
+        spread[:, s * cpties : (s + 1) * cpties] = (
+            tail[3:4, :cpties] + tail[4:5, :cpties] + tail[5:6, :cpties]
+        )
     me, core = place_ref[0], place_ref[1]
     slot = meta[0:1, :].astype(jnp.int32) ^ me
     slot = jnp.where(slot >= 2, slot ^ core, slot)
@@ -128,11 +169,11 @@
         delta[:, cols] = lax.dot_general(
             basis_ref[...], coef[cols, :], (((1,), (1,)), ((), ())), preferred_element_type=F32
         ).astype(BF16)
+    for cols in blocks:
+        r_all[:, cols] = dot(delta[...], m_hi[:, cols]) + dot(delta[...], m_lo[:, cols])
     squares = None
     for cols in blocks:
-        r = dot(delta[...], m_hi[:, cols]) + dot(delta[...], m_lo[:, cols])
-        r_all[:, cols] = r
-        hi, lo = split(delta[:, cols].astype(F32) * r)
+        hi, lo = split(delta[:, cols].astype(F32) * r_all[:, cols])
         part = dot(hi, group_hot[cols]) + dot(lo, group_hot[cols])
         squares = part if squares is None else squares + part
     margin = jnp.sqrt(squares + 1e-06)
@@ -172,23 +213,26 @@
     buckets = risk_weights.shape[0]
     paths, width = basis_values.shape
     trades = owners * per
-
-    def row(x):
-        return jnp.pad(x.astype(F32), (0, META_LANES - x.shape[0]))
-
-    meta = jnp.stack(
-        [
-            row(trade_cpty // cpties),
-            row(trade_cpty % cpties),
-            row(trade_bucket),
-            row(funding_spread),
-        ]
-    )
-    meta = jnp.pad(meta, ((0, 4), (0, 0)))
-    coef_all = gather_shards(coefficients, owners)
-    meta_all = gather_shards(meta, owners)
+    vmem = pl.BlockSpec(memory_space=pltpu.VMEM)
+    anywhere = pl.BlockSpec(memory_space=pl.ANY)
+
+    def pack(*refs):
+        pack_kernel(*refs, cpties=cpties)
+
+    payload = pl.pallas_call(
+        pack,
+        out_shape=jax.ShapeDtypeStruct((per + META_ROWS, width), BF16),
+        in_specs=[vmem, vmem, vmem, anywhere],
+        out_specs=anywhere,
+        scratch_shapes=[pltpu.VMEM((META_ROWS, width), F32), pltpu.SemaphoreType.DMA((2,))],
+    )(
+        trade_cpty.reshape(1, per),
+        trade_bucket.reshape(1, per),
+        funding_spread.reshape(1, cpties),
+        coefficients,
+    )
+    gathered = gather_shards(payload, owners)
     place = jnp.stack([lax.axis_index("trade"), lax.axis_index("path")]).astype(jnp.int32)
-    vmem = pl.BlockSpec(memory_space=pltpu.VMEM)
 
     def kernel(*refs):
         all_trades_kernel(*refs, shards=owners, per=per, cpties=cpties)
@@ -199,23 +243,22 @@
             jax.ShapeDtypeStruct((cpties, paths), F32),
             jax.ShapeDtypeStruct((paths, width), BF16),
         ],
-        in_specs=[pl.BlockSpec(memory_space=pltpu.SMEM)]
-        + [vmem] * (3 + owners)
-        + [pl.BlockSpec(memory_space=pl.ANY)] * owners,
+        in_specs=[pl.BlockSpec(memory_space=pltpu.SMEM)] + [vmem] * 3 + [anywhere] * owners,
         out_specs=[vmem, vmem],
         scratch_shapes=[
             pltpu.VMEM((trades, width), BF16),
-            pltpu.VMEM((8, trades), F32),
+            pltpu.VMEM((owners * META_ROWS, width), BF16),
+            pltpu.VMEM((META_ROWS, trades), F32),
             pltpu.VMEM((1, owners * cpties), F32),
             pltpu.VMEM((paths, trades), BF16),
             pltpu.VMEM((trades, trades), BF16),
             pltpu.VMEM((trades, trades), BF16),
             pltpu.VMEM((paths, trades), F32),
             pltpu.VMEM((paths, trades), BF16),
-            pltpu.SemaphoreType.DMA((owners,)),
+            pltpu.SemaphoreType.DMA((2 * owners,)),
         ],
-        compiler_params=pltpu.CompilerParams(vmem_limit_bytes=56 << 20),
-    )(place, basis_values, risk_weights.reshape(1, buckets), correlation, *meta_all, *coef_all)
+        compiler_params=pltpu.CompilerParams(vmem_limit_bytes=40 << 20),
+    )(place, basis_values, risk_weights.reshape(1, buckets), correlation, *gathered)
 
 
 def solution(mesh):

time: 54.3 us -> 43.2 us (0.80)
  starting transfers between devices: 16.6 us -> 7.9 us
  waiting for transfers between devices: 19.5 us -> 14.5 us
  Pallas kernels: 13.8 us -> 17.8 us
  other arithmetic: 1.37 us -> 0.07 us
    ppermute x8 -> x4, starting transfers between devices: 15.8 us -> 7.39 us  [fetch(): return lax.ppermute(x, ('trade', 'path'), pairs)]
    pallas_call x0 -> x1, Pallas kernels: none -> 6.81 us  [gather_body(): pl.pallas_call(pack, out_shape=jax.ShapeDtypeStruct((per + META_ROWS, wid...]
    ppermute x8 -> x4, waiting for transfers between devices: 16.9 us -> 13.4 us  [fetch(): return lax.ppermute(x, ('trade', 'path'), pairs)]
    pallas_call x1, Pallas kernels: 13.8 us -> 11 us  [gather_body(): pl.pallas_call(kernel, out_shape=[jax.ShapeDtypeStruct((cpties, paths), F...]
    ppermute x6 -> x3, waiting for transfers between devices: 2.52 us -> 1.05 us  [swap_cores(): return lax.ppermute(x, 'path', [(0, 1), (1, 0)])]
    convert_element_type x2 -> x0, other arithmetic: 0.69 us -> none  [row(): return jnp.pad(x.astype(F32), (0, META_LANES - x.shape[0]))]
    another operation x1, other arithmetic: 0.67 us -> 0.07 us  [gather_body(): jnp.stack([lax.axis_index('trade'), lax.axis_index('path')])]
    unnamed x34 -> x8, local copies, waits for them, and re-layouts: 2.07 us -> 1.97 us
  transfers between devices with their start and end apart: 14 -> 7, of which waited for: 10 -> 4; matrix products, arithmetic and copies ran while one was open for 3% -> 0% of each run, Pallas kernels for 0% -> 0%
where the time goes in v2:
time: 43.2 us; the launch traced here: 42.9 us
  Pallas kernels  17.8 us (41%)
  waiting for transfers between devices  14.5 us (34%)
  starting transfers between devices  7.9 us (18%)
  local copies, waits for them, and re-layouts  1.97 us (5%)
  between operations  0.66 us (2%)
    ppermute x4, waiting for transfers between devices, fetch(): return lax.ppermute(x, ('trade', 'path'), pairs)  13.4 us
    pallas_call x1, Pallas kernels, gather_body(): pl.pallas_call(kernel, out_shape=[jax.ShapeDtypeStruct((cpties, paths), F...  11 us
    ppermute x4, starting transfers between devices, fetch(): return lax.ppermute(x, ('trade', 'path'), pairs)  7.39 us
    pallas_call x1, Pallas kernels, gather_body(): pl.pallas_call(pack, out_shape=jax.ShapeDtypeStruct((per + META_ROWS, wid...  6.81 us
    unnamed x8, local copies, waits for them, and re-layouts  1.97 us
    ppermute x3, waiting for transfers between devices, swap_cores(): return lax.ppermute(x, 'path', [(0, 1), (1, 0)])  1.05 us
  transfers between devices with their start and end apart: 7, of which 4 were waited for; matrix products, arithmetic and copies ran while one was open for 0% of the time, Pallas kernels for 0%

profile of v2, /device:TPU:0, one launch (start us, length us, event | category | flops | bytes accessed | tf_op | source)
XLA Modules:
  0.0 42.9 jit_solution(5190084786645286177)
XLA Ops:
  0.6 0.0 copy-start.2
  0.6 6.8 %shard_map.86.refs_4_ = bf16[168,512]{1,0:T(8,128)(2,1)} custom-call(s32[1,160]{1,0:T(1,128)} %bitcast.7, s32[1,160]{1,0:T(1,128)} %bitcast.8, f32[1,16]{1,0:T(1,128)} %bitcast.9, bf16[160,512]{1,0:T(8,128)(2,1)} %refs_3_.2), custom_call_target="tpu_custom_call" | custom-call | tf_op jit(solution)/shard_map/pallas_call | solution.py:222
  7.5 5.1 %collective-permute-start.5 = (bf16[168,512]{1,0:T(8,128)(2,1)}, bf16[168,512]{1,0:T(8,128)(2,1)S(1)}, u32[]{:S(2)}, u32[]{:S(2)}) collective-permute-start(bf16[168,512]{1,0:T(8,128)(2,1)} %shard_map.86.refs_4_), channel_id=1, source_target_pairs={{0,12},{2,14},{4,8},{6,10},{8,4},{10,6},{12,0},{14,2},{1,15},{3,13... | collective-permute-start | bytes 516104 | tf_op jit(solution)/shard_map/ppermute | solution.py:196
  12.6 0.0 collective-permute-start.3
  12.6 0.6 %collective-permute-start.1 = (bf16[168,512]{1,0:T(8,128)(2,1)}, bf16[168,512]{1,0:T(8,128)(2,1)S(1)}, u32[]{:S(2)}, u32[]{:S(2)}) collective-permute-start(bf16[168,512]{1,0:T(8,128)(2,1)} %shard_map.86.refs_4_), channel_id=1, source_target_pairs={{0,4},{2,6},{4,0},{6,2},{8,12},{10,14},{12,8},{14,10},{1,7},{3,5},... | collective-permute-start | bytes 516104 | tf_op jit(solution)/shard_map/ppermute | solution.py:196
  13.2 1.6 %collective-permute-start = (bf16[168,512]{1,0:T(8,128)(2,1)}, bf16[168,512]{1,0:T(8,128)(2,1)S(1)}, u32[]{:S(2)}, u32[]{:S(2)}) collective-permute-start(bf16[168,512]{1,0:T(8,128)(2,1)} %shard_map.86.refs_4_), channel_id=1, source_target_pairs={{0,2},{2,0},{4,6},{6,4},{8,10},{10,8},{12,14},{14,12},{1,3},{3,1},... | collective-permute-start | bytes 516104 | tf_op jit(solution)/shard_map/ppermute | solution.py:196
  14.9 3.4 %collective-permute-done.5.refs_10_ = bf16[168,512]{1,0:T(8,128)(2,1)S(1)} collective-permute-done((bf16[168,512]{1,0:T(8,128)(2,1)}, bf16[168,512]{1,0:T(8,128)(2,1)S(1)}, u32[]{:S(2)}, u32[]{:S(2)}) %collective-permute-start.5) | collective-permute-done | bytes 172064 | tf_op jit(solution)/shard_map/ppermute | solution.py:196
  18.2 0.0 collective-permute-start.6
  18.2 10.1 %collective-permute-done.3.refs_8_ = bf16[168,512]{1,0:T(8,128)(2,1)S(1)} collective-permute-done((bf16[168,512]{1,0:T(8,128)(2,1)}, bf16[168,512]{1,0:T(8,128)(2,1)S(1)}, u32[]{:S(2)}, u32[]{:S(2)}) %collective-permute-start.3) | collective-permute-done | bytes 172064 | tf_op jit(solution)/shard_map/ppermute | solution.py:196
  28.3 0.0 collective-permute-start.4
  28.3 0.0 collective-permute-done.1.refs_6_
  28.3 0.5 %collective-permute-start.2 = (bf16[168,512]{1,0:T(8,128)(2,1)S(1)}, bf16[168,512]{1,0:T(8,128)(2,1)S(1)}, u32[]{:S(2)}, u32[]{:S(2)}) collective-permute-start(bf16[168,512]{1,0:T(8,128)(2,1)S(1)} %collective-permute-done.1.refs_6_), channel_id=1, source_target_pairs={{0,1},{1,0},{2,3},{3,2},{4,5},{5,4},{6,7},{7,6},{8,9},{9,8},{10,11... | collective-permute-start | bytes 516104 | tf_op jit(solution)/shard_map/ppermute | solution.py:190
  28.8 0.1 pad_add_fusion.refs_0_
  28.9 0.0 copy-start.3
  28.9 0.0 collective-permute-done.refs_5_
  28.9 0.0 collective-permute-done.6.refs_11_
  28.9 0.8 %collective-permute-done.4.refs_9_ = bf16[168,512]{1,0:T(8,128)(2,1)S(1)} collective-permute-done((bf16[168,512]{1,0:T(8,128)(2,1)S(1)}, bf16[168,512]{1,0:T(8,128)(2,1)S(1)}, u32[]{:S(2)}, u32[]{:S(2)}) %collective-permute-start.4) | collective-permute-done | bytes 172064 | tf_op jit(solution)/shard_map/ppermute | solution.py:190
  29.7 0.2 collective-permute-done.2.refs_7_
  29.9 0.0 copy-done.2
  30.0 0.0 copy-done.3
  30.0 0.0 copy-start
  30.0 0.9 %copy-done = bf16[168,512]{1,0:T(8,128)(2,1)S(1)} copy-done((bf16[168,512]{1,0:T(8,128)(2,1)S(1)}, bf16[168,512]{1,0:T(8,128)(2,1)}, u32[]{:S(2)}) %copy-start) | copy-done | bytes 172056
  30.9 0.0 copy-start.1
  30.9 1.0 %copy-done.1 = bf16[512,512]{1,0:T(8,128)(2,1)S(1)} copy-done((bf16[512,512]{1,0:T(8,128)(2,1)S(1)}, bf16[512,512]{1,0:T(8,128)(2,1)}, u32[]{:S(2)}) %copy-start.1) | copy-done | bytes 524312
  31.9 11.0 %shard_map.87 = (f32[16,512]{1,0:T(8,128)}, bf16[512,512]{1,0:T(8,128)(2,1)}) custom-call(s32[2]{0:T(128)S(1)} %pad_add_fusion.refs_0_, bf16[512,512]{1,0:T(8,128)(2,1)S(1)} %copy-done.1, f32[1,128]{1,0:T(1,128)S(1)} %bitcast.6, f32[128,128]{1,0:T(8,128)S(1)} %copy-done.2, bf16[168,512]{1,0:T(8,128)(2,1)S(1)} %copy-done, ...), custom_call_target="tpu_custom_call" | custom-call | tf_op jit(solution)/shard_map/pallas_call | solution.py:240
Async XLA Ops:
  0.6 29.3 %copy-start.2 = (f32[128,128]{1,0:T(8,128)S(1)}, f32[128,128]{1,0:T(8,128)}, u32[]{:S(2)}) copy-start(f32[128,128]{1,0:T(8,128)} %refs_3_.3) | copy-start | bytes 196612
  7.5 10.7 %collective-permute-start.5 = (bf16[168,512]{1,0:T(8,128)(2,1)}, bf16[168,512]{1,0:T(8,128)(2,1)S(1)}, u32[]{:S(2)}, u32[]{:S(2)}) collective-permute-start(bf16[168,512]{1,0:T(8,128)(2,1)} %shard_map.86.refs_4_), channel_id=1, source_target_pairs={{0,12},{2,14},{4,8},{6,10},{8,4},{10,6},{12,0},{14,2},{1,15},{3,13... | collective-permute-start | bytes 516104 | tf_op jit(solution)/shard_map/ppermute | solution.py:196
  12.6 15.7 %collective-permute-start.3 = (bf16[168,512]{1,0:T(8,128)(2,1)}, bf16[168,512]{1,0:T(8,128)(2,1)S(1)}, u32[]{:S(2)}, u32[]{:S(2)}) collective-permute-start(bf16[168,512]{1,0:T(8,128)(2,1)} %shard_map.86.refs_4_), channel_id=1, source_target_pairs={{0,8},{2,10},{4,12},{6,14},{8,0},{10,2},{12,4},{14,6},{1,11},{3,9}... | collective-permute-start | bytes 516104 | tf_op jit(solution)/shard_map/ppermute | solution.py:196
  12.6 15.7 %collective-permute-start.1 = (bf16[168,512]{1,0:T(8,128)(2,1)}, bf16[168,512]{1,0:T(8,128)(2,1)S(1)}, u32[]{:S(2)}, u32[]{:S(2)}) collective-permute-start(bf16[168,512]{1,0:T(8,128)(2,1)} %shard_map.86.refs_4_), channel_id=1, source_target_pairs={{0,4},{2,6},{4,0},{6,2},{8,12},{10,14},{12,8},{14,10},{1,7},{3,5},... | collective-permute-start | bytes 516104 | tf_op jit(solution)/shard_map/ppermute | solution.py:196
  13.2 15.7 %collective-permute-start = (bf16[168,512]{1,0:T(8,128)(2,1)}, bf16[168,512]{1,0:T(8,128)(2,1)S(1)}, u32[]{:S(2)}, u32[]{:S(2)}) collective-permute-start(bf16[168,512]{1,0:T(8,128)(2,1)} %shard_map.86.refs_4_), channel_id=1, source_target_pairs={{0,2},{2,0},{4,6},{6,4},{8,10},{10,8},{12,14},{14,12},{1,3},{3,1},... | collective-permute-start | bytes 516104 | tf_op jit(solution)/shard_map/ppermute | solution.py:196
  18.2 10.7 %collective-permute-start.6 = (bf16[168,512]{1,0:T(8,128)(2,1)S(1)}, bf16[168,512]{1,0:T(8,128)(2,1)S(1)}, u32[]{:S(2)}, u32[]{:S(2)}) collective-permute-start(bf16[168,512]{1,0:T(8,128)(2,1)S(1)} %collective-permute-done.5.refs_10_), channel_id=1, source_target_pairs={{0,1},{1,0},{2,3},{3,2},{4,5},{5,4},{6,7},{7,6},{8,9},{9,8},{10,11... | collective-permute-start | bytes 516104 | tf_op jit(solution)/shard_map/ppermute | solution.py:190
  28.3 1.4 %collective-permute-start.4 = (bf16[168,512]{1,0:T(8,128)(2,1)S(1)}, bf16[168,512]{1,0:T(8,128)(2,1)S(1)}, u32[]{:S(2)}, u32[]{:S(2)}) collective-permute-start(bf16[168,512]{1,0:T(8,128)(2,1)S(1)} %collective-permute-done.3.refs_8_), channel_id=1, source_target_pairs={{0,1},{1,0},{2,3},{3,2},{4,5},{5,4},{6,7},{7,6},{8,9},{9,8},{10,11... | collective-permute-start | bytes 516104 | tf_op jit(solution)/shard_map/ppermute | solution.py:190
  28.3 1.6 %collective-permute-start.2 = (bf16[168,512]{1,0:T(8,128)(2,1)S(1)}, bf16[168,512]{1,0:T(8,128)(2,1)S(1)}, u32[]{:S(2)}, u32[]{:S(2)}) collective-permute-start(bf16[168,512]{1,0:T(8,128)(2,1)S(1)} %collective-permute-done.1.refs_6_), channel_id=1, source_target_pairs={{0,1},{1,0},{2,3},{3,2},{4,5},{5,4},{6,7},{7,6},{8,9},{9,8},{10,11... | collective-permute-start | bytes 516104 | tf_op jit(solution)/shard_map/ppermute | solution.py:190
  28.9 1.1 %copy-start.3 = (f32[128]{0:T(128)S(1)}, f32[128]{0:T(128)}, u32[]{:S(2)}) copy-start(f32[128]{0:T(128)} %param.11) | copy-start | bytes 1540
  30.0 0.9 %copy-start = (bf16[168,512]{1,0:T(8,128)(2,1)S(1)}, bf16[168,512]{1,0:T(8,128)(2,1)}, u32[]{:S(2)}) copy-start(bf16[168,512]{1,0:T(8,128)(2,1)} %shard_map.86.refs_4_) | copy-start | bytes 516100
  30.9 1.0 %copy-start.1 = (bf16[512,512]{1,0:T(8,128)(2,1)S(1)}, bf16[512,512]{1,0:T(8,128)(2,1)}, u32[]{:S(2)}) copy-start(bf16[512,512]{1,0:T(8,128)(2,1)} %refs_1_.1) | copy-start | bytes 1572868

commit v3 on v2

--- a/solution.py
+++ b/solution.py
@@ -81,10 +81,9 @@
     return (ids == row).astype(F32).astype(BF16)
 
 
-def pack_kernel(cpty_ref, bucket_ref, spread_ref, coef_ref, out_ref, meta, sem, *, cpties):
-    per, width = coef_ref.shape
-    body = pltpu.make_async_copy(coef_ref, out_ref.at[pl.ds(0, per)], sem.at[0])
-    body.start()
+def pack_kernel(cpty_ref, bucket_ref, spread_ref, coef_ref, out_ref, meta, *, cpties):
+    per = coef_ref.shape[0]
+    rows = meta.shape[0]
     cpty = cpty_ref[...]
     owner = cpty // cpties
     meta[...] = jnp.zeros_like(meta)
@@ -97,39 +96,49 @@
     meta[3:4, :cpties] = high
     meta[4:5, :cpties] = middle
     meta[5:6, :cpties] = spread - high - middle
-    rows = meta.shape[0]
-
-    def tail(block):
-        block[...] = meta[...].astype(BF16)
-        copy = pltpu.make_async_copy(block, out_ref.at[pl.ds(per, rows)], sem.at[1])
-        copy.start()
-        copy.wait()
-
-    pl.run_scoped(tail, pltpu.VMEM((rows, width), BF16))
-    body.wait()
-
-
-def all_trades_kernel(place_ref, basis_ref, weight_ref, corr_ref, *refs, shards, per, cpties):
-    shard_refs = refs[:shards]
-    margin_ref, adj_ref = refs[shards : shards + 2]
-    coef, tails, meta, spread, delta, m_hi, m_lo, r_all, bar, sem = refs[shards + 2 :]
+    out_ref[:per] = coef_ref[...]
+    out_ref[per : per + rows] = meta[...].astype(BF16)
+
+
+def all_trades_kernel(basis_ref, weight_ref, corr_ref, *refs, shards, per, cpties):
+    both, ends = refs[: shards - 1], refs[shards - 1 : shards + 1]
+    margin_ref, adj_ref = refs[shards + 1 : shards + 3]
+    basis, coef, tails, meta, spread, delta, m_hi, m_lo, r_all, bar, sem = refs[shards + 3 :]
     trades = shards * per
     groups = shards * cpties
     buckets = corr_ref.shape[0]
-    heads = [
-        pltpu.make_async_copy(
-            shard_refs[s].at[pl.ds(per, META_ROWS)], tails.at[pl.ds(s * META_ROWS, META_ROWS)], sem.at[s]
+    me, core = lax.axis_index("trade"), lax.axis_index("path")
+
+    def shard_copies(s, ref):
+        head = pltpu.make_async_copy(
+            ref.at[pl.ds(per, META_ROWS)], tails.at[pl.ds(s * META_ROWS, META_ROWS)], sem.at[s]
         )
-        for s in range(shards)
-    ]
-    copies = [
-        pltpu.make_async_copy(
-            shard_refs[s].at[pl.ds(0, per)], coef.at[pl.ds(s * per, per)], sem.at[shards + s]
+        body = pltpu.make_async_copy(
+            ref.at[pl.ds(0, per)], coef.at[pl.ds(s * per, per)], sem.at[shards + s]
         )
-        for s in range(shards)
-    ]
-    for copy in heads + copies:
-        copy.start()
+        return head, body
+
+    heads, copies = [], []
+    for s, ref in enumerate(both):
+        head, body = shard_copies(s, ref)
+        head.start()
+        body.start()
+        heads.append(head)
+        copies.append(body)
+    for k in range(1):
+        s = len(both) + k
+        for side in range(2):
+
+            @pl.when(core == side)
+            def _():
+                for copy in shard_copies(s, ends[2 * k + side]):
+                    copy.start()
+
+        head, body = shard_copies(s, ends[2 * k])
+        heads.append(head)
+        copies.append(body)
+    copies.append(pltpu.make_async_copy(basis_ref, basis, sem.at[2 * shards]))
+    copies[-1].start()
     for copy in heads:
         copy.wait()
     for s in range(shards):
@@ -138,10 +147,11 @@
         spread[:, s * cpties : (s + 1) * cpties] = (
             tail[3:4, :cpties] + tail[4:5, :cpties] + tail[5:6, :cpties]
         )
-    me, core = place_ref[0], place_ref[1]
-    slot = meta[0:1, :].astype(jnp.int32) ^ me
-    slot = jnp.where(slot >= 2, slot ^ core, slot)
-    group = (slot * cpties).astype(F32) + meta[1:2, :]
+    offset = meta[0:1, :].astype(jnp.int32) ^ me
+    group = meta[1:2, :]
+    for s in range(1, shards):
+        there = jnp.where(core == 0, LAYOUT[0][s], LAYOUT[1][s])
+        group = group + jnp.where(offset == there, F32(s * cpties), F32(0))
     bucket = meta[2:3, :]
     group_t = one_hot_t(group, groups)
     group_hot = group_t.T
@@ -167,7 +177,7 @@
         copy.wait()
     for cols in blocks:
         delta[:, cols] = lax.dot_general(
-            basis_ref[...], coef[cols, :], (((1,), (1,)), ((), ())), preferred_element_type=F32
+            basis[...], coef[cols, :], (((1,), (1,)), ((), ())), preferred_element_type=F32
         ).astype(BF16)
     for cols in blocks:
         r_all[:, cols] = dot(delta[...], m_hi[:, cols]) + dot(delta[...], m_lo[:, cols])
@@ -190,18 +200,26 @@
     return lax.ppermute(x, "path", [(0, 1), (1, 0)])
 
 
-def fetch(x, first, second, owners):
-    pairs = [(i * 2, (i ^ first) * 2) for i in range(owners)]
-    pairs += [(i * 2 + 1, (i ^ second) * 2 + 1) for i in range(owners)]
+def fetch(x, owners, *offsets):
+    pairs = []
+    for core, offset in enumerate(offsets):
+        pairs += [((i ^ offset) * 2 + core, i * 2 + core) for i in range(owners)]
     return lax.ppermute(x, ("trade", "path"), pairs)
 
 
+LAYOUT = ((0, 4, 2, 5, 3, 6, 7, 1), (0, 2, 4, 3, 5, 7, 6, 1))
+
+
 def gather_shards(x, owners):
-    far = fetch(x, 4, 5, owners)
-    farther = fetch(x, 6, 7, owners)
-    near = fetch(x, 2, 3, owners)
-    beside = fetch(x, 1, 1, owners)
-    return [x, beside, near, swap_cores(near), far, swap_cores(far), farther, swap_cores(farther)]
+    first = fetch(x, owners, 4, 2)
+    beside = fetch(x, owners, 0, 1)
+    beside, first = lax.optimization_barrier((beside, first))
+    first_other = swap_cores(first)
+    second = fetch(first, owners, 1, 1)
+    opposite = jnp.where(lax.axis_index("path") == 0, first, first_other)
+    third = fetch(opposite, owners, 2, 3)
+    both = [x, first, first_other, second, swap_cores(second), third, swap_cores(third)]
+    return both + [swap_cores(beside), beside]
 
 
 def gather_body(
@@ -222,9 +240,9 @@
     payload = pl.pallas_call(
         pack,
         out_shape=jax.ShapeDtypeStruct((per + META_ROWS, width), BF16),
-        in_specs=[vmem, vmem, vmem, anywhere],
-        out_specs=anywhere,
-        scratch_shapes=[pltpu.VMEM((META_ROWS, width), F32), pltpu.SemaphoreType.DMA((2,))],
+        in_specs=[vmem] * 4,
+        out_specs=vmem,
+        scratch_shapes=[pltpu.VMEM((META_ROWS, width), F32)],
     )(
         trade_cpty.reshape(1, per),
         trade_bucket.reshape(1, per),
@@ -232,7 +250,6 @@
         coefficients,
     )
     gathered = gather_shards(payload, owners)
-    place = jnp.stack([lax.axis_index("trade"), lax.axis_index("path")]).astype(jnp.int32)
 
     def kernel(*refs):
         all_trades_kernel(*refs, shards=owners, per=per, cpties=cpties)
@@ -243,9 +260,11 @@
             jax.ShapeDtypeStruct((cpties, paths), F32),
             jax.ShapeDtypeStruct((paths, width), BF16),
         ],
-        in_specs=[pl.BlockSpec(memory_space=pltpu.SMEM)] + [vmem] * 3 + [anywhere] * owners,
+        in_specs=[pl.BlockSpec(memory_space=pltpu.HBM), vmem, vmem]
+        + [anywhere] * len(gathered),
         out_specs=[vmem, vmem],
         scratch_shapes=[
+            pltpu.VMEM((paths, width), BF16),
             pltpu.VMEM((trades, width), BF16),
             pltpu.VMEM((owners * META_ROWS, width), BF16),
             pltpu.VMEM((META_ROWS, trades), F32),
@@ -255,10 +274,10 @@
             pltpu.VMEM((trades, trades), BF16),
             pltpu.VMEM((paths, trades), F32),
             pltpu.VMEM((paths, trades), BF16),
-            pltpu.SemaphoreType.DMA((2 * owners,)),
+            pltpu.SemaphoreType.DMA((2 * owners + 1,)),
         ],
         compiler_params=pltpu.CompilerParams(vmem_limit_bytes=40 << 20),
-    )(place, basis_values, risk_weights.reshape(1, buckets), correlation, *gathered)
+    )(basis_values, risk_weights.reshape(1, buckets), correlation, *gathered)
 
 
 def solution(mesh):

time: 43.2 us -> 32.1 us (0.74)
  waiting for transfers between devices: 14.5 us -> 8.65 us
  Pallas kernels: 17.8 us -> 12.3 us
  starting transfers between devices: 7.9 us -> 10.4 us
  local copies, waits for them, and re-layouts: 1.97 us -> 0.02 us
    ppermute x4, waiting for transfers between devices: 13.4 us -> 7.28 us  [fetch(): return lax.ppermute(x, ('trade', 'path'), pairs)]
    pallas_call x1, Pallas kernels: 6.81 us -> 1.71 us  [gather_body(): pl.pallas_call(pack, out_shape=jax.ShapeDtypeStruct((per + META_ROWS, wid...]
    unnamed x8, local copies, waits for them, and re-layouts: 1.97 us -> 0.02 us
    ppermute x4, starting transfers between devices: 7.39 us -> 8.89 us  [fetch(): return lax.ppermute(x, ('trade', 'path'), pairs)]
    ppermute x3 -> x4, starting transfers between devices: 0.51 us -> 1.48 us  [swap_cores(): return lax.ppermute(x, 'path', [(0, 1), (1, 0)])]
    pallas_call x1, Pallas kernels: 11 us -> 10.5 us  [gather_body(): pl.pallas_call(kernel, out_shape=[jax.ShapeDtypeStruct((cpties, paths), F...]
    ppermute x3 -> x4, waiting for transfers between devices: 1.05 us -> 1.36 us  [swap_cores(): return lax.ppermute(x, 'path', [(0, 1), (1, 0)])]
  transfers between devices with their start and end apart: 7 -> 8, of which waited for: 4 -> 5; matrix products, arithmetic and copies ran while one was open for 0% -> 0% of each run, Pallas kernels for 0% -> 0%
where the time goes in v3:
time: 32.1 us; the launch traced here: 32 us
  Pallas kernels  12.3 us (38%)
  starting transfers between devices  10.4 us (32%)
  waiting for transfers between devices  8.65 us (27%)
  between operations  0.67 us (2%)
    pallas_call x1, Pallas kernels, gather_body(): pl.pallas_call(kernel, out_shape=[jax.ShapeDtypeStruct((cpties, paths), F...  10.5 us
    ppermute x4, starting transfers between devices, fetch(): return lax.ppermute(x, ('trade', 'path'), pairs)  8.89 us
    ppermute x4, waiting for transfers between devices, fetch(): return lax.ppermute(x, ('trade', 'path'), pairs)  7.28 us
    pallas_call x1, Pallas kernels, gather_body(): pl.pallas_call(pack, out_shape=jax.ShapeDtypeStruct((per + META_ROWS, wid...  1.71 us
    ppermute x4, starting transfers between devices, swap_cores(): return lax.ppermute(x, 'path', [(0, 1), (1, 0)])  1.48 us
    ppermute x4, waiting for transfers between devices, swap_cores(): return lax.ppermute(x, 'path', [(0, 1), (1, 0)])  1.36 us
  transfers between devices with their start and end apart: 8, of which 5 were waited for; matrix products, arithmetic and copies ran while one was open for 0% of the time, Pallas kernels for 0%

profile of v3, /device:TPU:0, one launch (start us, length us, event | category | flops | bytes accessed | tf_op | source)
XLA Modules:
  0.0 32.0 jit_solution(1211418889004380549)
XLA Ops:
  0.6 0.0 copy-start.1
  0.6 1.7 %shard_map.86.refs_3_ = bf16[168,512]{1,0:T(8,128)(2,1)} custom-call(s32[1,160]{1,0:T(1,128)} %bitcast.5, s32[1,160]{1,0:T(1,128)} %bitcast.6, f32[1,16]{1,0:T(1,128)} %bitcast.7, bf16[160,512]{1,0:T(8,128)(2,1)} %refs_3_.1), custom_call_target="tpu_custom_call" | custom-call | tf_op jit(solution)/shard_map/pallas_call | solution.py:240
  2.4 4.0 %collective-permute-start.1 = (bf16[168,512]{1,0:T(8,128)(2,1)}, bf16[168,512]{1,0:T(8,128)(2,1)S(1)}, u32[]{:S(2)}, u32[]{:S(2)}) collective-permute-start(bf16[168,512]{1,0:T(8,128)(2,1)} %shard_map.86.refs_3_), channel_id=1, source_target_pairs={{8,0},{10,2},{12,4},{14,6},{0,8},{2,10},{4,12},{6,14},{5,1},{7,3},... | collective-permute-start | bytes 516104 | tf_op jit(solution)/shard_map/ppermute | solution.py:207
  6.4 1.6 %collective-permute-start = (bf16[168,512]{1,0:T(8,128)(2,1)}, bf16[168,512]{1,0:T(8,128)(2,1)S(1)}, u32[]{:S(2)}, u32[]{:S(2)}) collective-permute-start(bf16[168,512]{1,0:T(8,128)(2,1)} %shard_map.86.refs_3_), channel_id=1, source_target_pairs={{0,0},{2,2},{4,4},{6,6},{8,8},{10,10},{12,12},{14,14},{3,1},{1,3},... | collective-permute-start | bytes 516104 | tf_op jit(solution)/shard_map/ppermute | solution.py:207
  8.0 2.5 %collective-permute-done.1.refs_4_ = bf16[168,512]{1,0:T(8,128)(2,1)S(1)} collective-permute-done((bf16[168,512]{1,0:T(8,128)(2,1)}, bf16[168,512]{1,0:T(8,128)(2,1)S(1)}, u32[]{:S(2)}, u32[]{:S(2)}) %collective-permute-start.1) | collective-permute-done | bytes 172064 | tf_op jit(solution)/shard_map/ppermute | solution.py:207
  10.5 0.0 collective-permute-done.refs_11_
  10.5 0.8 %collective-permute-start.2 = (bf16[168,512]{1,0:T(8,128)(2,1)S(1)}, bf16[168,512]{1,0:T(8,128)(2,1)S(1)}, u32[]{:S(2)}, u32[]{:S(2)}) collective-permute-start(bf16[168,512]{1,0:T(8,128)(2,1)S(1)} %collective-permute-done.1.refs_4_), channel_id=1, source_target_pairs={{0,1},{1,0},{2,3},{3,2},{4,5},{5,4},{6,7},{7,6},{8,9},{9,8},{10,11... | collective-permute-start | bytes 516104 | tf_op jit(solution)/shard_map/ppermute | solution.py:200
  11.3 0.0 copy-start
  11.3 0.0 copy-start.2
  11.3 1.5 %collective-permute-start.3 = (bf16[168,512]{1,0:T(8,128)(2,1)S(1)}, bf16[168,512]{1,0:T(8,128)(2,1)S(1)}, u32[]{:S(2)}, u32[]{:S(2)}) collective-permute-start(bf16[168,512]{1,0:T(8,128)(2,1)S(1)} %collective-permute-done.1.refs_4_), channel_id=1, source_target_pairs={{2,0},{0,2},{6,4},{4,6},{10,8},{8,10},{14,12},{12,14},{3,1},{1,3},... | collective-permute-start | bytes 516104 | tf_op jit(solution)/shard_map/ppermute | solution.py:207
  12.8 0.0 collective-permute-done.2.refs_5_
  12.8 0.0 copy-start.3
  12.8 1.8 %collective-permute-start.5 = (bf16[168,512]{1,0:T(8,128)(2,1)S(1)}, bf16[168,512]{1,0:T(8,128)(2,1)S(1)}, u32[]{:S(2)}, u32[]{:S(2)}) collective-permute-start(bf16[168,512]{1,0:T(8,128)(2,1)S(1)} %broadcast_select_fusion), channel_id=1, source_target_pairs={{4,0},{6,2},{0,4},{2,6},{12,8},{14,10},{8,12},{10,14},{7,1},{5,3},... | collective-permute-start | bytes 516104 | tf_op jit(solution)/shard_map/ppermute | solution.py:207
  14.6 0.6 %collective-permute-start.7 = (bf16[168,512]{1,0:T(8,128)(2,1)S(1)}, bf16[168,512]{1,0:T(8,128)(2,1)S(1)}, u32[]{:S(2)}, u32[]{:S(2)}) collective-permute-start(bf16[168,512]{1,0:T(8,128)(2,1)S(1)} %collective-permute-done.refs_11_), channel_id=1, source_target_pairs={{0,1},{1,0},{2,3},{3,2},{4,5},{5,4},{6,7},{7,6},{8,9},{9,8},{10,11... | collective-permute-start | bytes 516104 | tf_op jit(solution)/shard_map/ppermute | solution.py:200
  15.2 4.3 %collective-permute-done.3.refs_6_ = bf16[168,512]{1,0:T(8,128)(2,1)S(1)} collective-permute-done((bf16[168,512]{1,0:T(8,128)(2,1)S(1)}, bf16[168,512]{1,0:T(8,128)(2,1)S(1)}, u32[]{:S(2)}, u32[]{:S(2)}) %collective-permute-start.3) | collective-permute-done | bytes 172064 | tf_op jit(solution)/shard_map/ppermute | solution.py:207
  19.5 0.0 collective-permute-start.4
  19.5 0.5 %collective-permute-done.5.refs_8_ = bf16[168,512]{1,0:T(8,128)(2,1)S(1)} collective-permute-done((bf16[168,512]{1,0:T(8,128)(2,1)S(1)}, bf16[168,512]{1,0:T(8,128)(2,1)S(1)}, u32[]{:S(2)}, u32[]{:S(2)}) %collective-permute-start.5) | collective-permute-done | bytes 172064 | tf_op jit(solution)/shard_map/ppermute | solution.py:207
  20.0 0.0 collective-permute-start.6
  20.1 0.0 collective-permute-done.7.refs_10_
  20.1 0.9 %collective-permute-done.4.refs_7_ = bf16[168,512]{1,0:T(8,128)(2,1)S(1)} collective-permute-done((bf16[168,512]{1,0:T(8,128)(2,1)S(1)}, bf16[168,512]{1,0:T(8,128)(2,1)S(1)}, u32[]{:S(2)}, u32[]{:S(2)}) %collective-permute-start.4) | collective-permute-done | bytes 172064 | tf_op jit(solution)/shard_map/ppermute | solution.py:200
  20.9 0.5 %collective-permute-done.6.refs_9_ = bf16[168,512]{1,0:T(8,128)(2,1)S(1)} collective-permute-done((bf16[168,512]{1,0:T(8,128)(2,1)S(1)}, bf16[168,512]{1,0:T(8,128)(2,1)S(1)}, u32[]{:S(2)}, u32[]{:S(2)}) %collective-permute-start.6) | collective-permute-done | bytes 172064 | tf_op jit(solution)/shard_map/ppermute | solution.py:200
  21.4 0.0 copy-done.1
  21.4 0.0 copy-done
  21.4 0.0 copy-done.2
  21.4 0.0 copy-done.3
  21.4 10.5 %shard_map.87 = (f32[16,512]{1,0:T(8,128)}, bf16[512,512]{1,0:T(8,128)(2,1)}) custom-call(bf16[512,512]{1,0:T(8,128)(2,1)S(1)} %copy-done.1, f32[1,128]{1,0:T(1,128)S(1)} %bitcast.4, f32[128,128]{1,0:T(8,128)S(1)} %copy-done.2, bf16[168,512]{1,0:T(8,128)(2,1)S(1)} %copy-done, bf16[168,512]{1,0:T(8,128)(2,1)S(1)} %collective-permute-done.1.refs_4_, ...), custom_call_target="tpu_custom_call" | custom-call | tf_op jit(solution)/shard_map/pallas_call | solution.py:257
  (1 shorter events, 0.0 us)
Async XLA Ops:
  0.6 20.8 %copy-start.1 = (bf16[512,512]{1,0:T(8,128)(2,1)S(1)}, bf16[512,512]{1,0:T(8,128)(2,1)}, u32[]{:S(2)}) copy-start(bf16[512,512]{1,0:T(8,128)(2,1)} %refs_0_.1) | copy-start | bytes 1572868
  2.4 8.1 %collective-permute-start.1 = (bf16[168,512]{1,0:T(8,128)(2,1)}, bf16[168,512]{1,0:T(8,128)(2,1)S(1)}, u32[]{:S(2)}, u32[]{:S(2)}) collective-permute-start(bf16[168,512]{1,0:T(8,128)(2,1)} %shard_map.86.refs_3_), channel_id=1, source_target_pairs={{8,0},{10,2},{12,4},{14,6},{0,8},{2,10},{4,12},{6,14},{5,1},{7,3},... | collective-permute-start | bytes 516104 | tf_op jit(solution)/shard_map/ppermute | solution.py:207
  6.4 4.1 %collective-permute-start = (bf16[168,512]{1,0:T(8,128)(2,1)}, bf16[168,512]{1,0:T(8,128)(2,1)S(1)}, u32[]{:S(2)}, u32[]{:S(2)}) collective-permute-start(bf16[168,512]{1,0:T(8,128)(2,1)} %shard_map.86.refs_3_), channel_id=1, source_target_pairs={{0,0},{2,2},{4,4},{6,6},{8,8},{10,10},{12,12},{14,14},{3,1},{1,3},... | collective-permute-start | bytes 516104 | tf_op jit(solution)/shard_map/ppermute | solution.py:207
  10.5 2.3 %collective-permute-start.2 = (bf16[168,512]{1,0:T(8,128)(2,1)S(1)}, bf16[168,512]{1,0:T(8,128)(2,1)S(1)}, u32[]{:S(2)}, u32[]{:S(2)}) collective-permute-start(bf16[168,512]{1,0:T(8,128)(2,1)S(1)} %collective-permute-done.1.refs_4_), channel_id=1, source_target_pairs={{0,1},{1,0},{2,3},{3,2},{4,5},{5,4},{6,7},{7,6},{8,9},{9,8},{10,11... | collective-permute-start | bytes 516104 | tf_op jit(solution)/shard_map/ppermute | solution.py:200
  11.3 10.1 %copy-start = (bf16[168,512]{1,0:T(8,128)(2,1)S(1)}, bf16[168,512]{1,0:T(8,128)(2,1)}, u32[]{:S(2)}) copy-start(bf16[168,512]{1,0:T(8,128)(2,1)} %shard_map.86.refs_3_) | copy-start | bytes 516100
  11.3 10.1 %copy-start.2 = (f32[128,128]{1,0:T(8,128)S(1)}, f32[128,128]{1,0:T(8,128)}, u32[]{:S(2)}) copy-start(f32[128,128]{1,0:T(8,128)} %refs_2_.1) | copy-start | bytes 196612
  11.3 8.2 %collective-permute-start.3 = (bf16[168,512]{1,0:T(8,128)(2,1)S(1)}, bf16[168,512]{1,0:T(8,128)(2,1)S(1)}, u32[]{:S(2)}, u32[]{:S(2)}) collective-permute-start(bf16[168,512]{1,0:T(8,128)(2,1)S(1)} %collective-permute-done.1.refs_4_), channel_id=1, source_target_pairs={{2,0},{0,2},{6,4},{4,6},{10,8},{8,10},{14,12},{12,14},{3,1},{1,3},... | collective-permute-start | bytes 516104 | tf_op jit(solution)/shard_map/ppermute | solution.py:207
  12.8 8.6 %copy-start.3 = (f32[128]{0:T(128)S(1)}, f32[128]{0:T(128)}, u32[]{:S(2)}) copy-start(f32[128]{0:T(128)} %param.11) | copy-start | bytes 1540
  12.8 7.2 %collective-permute-start.5 = (bf16[168,512]{1,0:T(8,128)(2,1)S(1)}, bf16[168,512]{1,0:T(8,128)(2,1)S(1)}, u32[]{:S(2)}, u32[]{:S(2)}) collective-permute-start(bf16[168,512]{1,0:T(8,128)(2,1)S(1)} %broadcast_select_fusion), channel_id=1, source_target_pairs={{4,0},{6,2},{0,4},{2,6},{12,8},{14,10},{8,12},{10,14},{7,1},{5,3},... | collective-permute-start | bytes 516104 | tf_op jit(solution)/shard_map/ppermute | solution.py:207
  14.6 5.4 %collective-permute-start.7 = (bf16[168,512]{1,0:T(8,128)(2,1)S(1)}, bf16[168,512]{1,0:T(8,128)(2,1)S(1)}, u32[]{:S(2)}, u32[]{:S(2)}) collective-permute-start(bf16[168,512]{1,0:T(8,128)(2,1)S(1)} %collective-permute-done.refs_11_), channel_id=1, source_target_pairs={{0,1},{1,0},{2,3},{3,2},{4,5},{5,4},{6,7},{7,6},{8,9},{9,8},{10,11... | collective-permute-start | bytes 516104 | tf_op jit(solution)/shard_map/ppermute | solution.py:200
  19.5 1.4 %collective-permute-start.4 = (bf16[168,512]{1,0:T(8,128)(2,1)S(1)}, bf16[168,512]{1,0:T(8,128)(2,1)S(1)}, u32[]{:S(2)}, u32[]{:S(2)}) collective-permute-start(bf16[168,512]{1,0:T(8,128)(2,1)S(1)} %collective-permute-done.3.refs_6_), channel_id=1, source_target_pairs={{0,1},{1,0},{2,3},{3,2},{4,5},{5,4},{6,7},{7,6},{8,9},{9,8},{10,11... | collective-permute-start | bytes 516104 | tf_op jit(solution)/shard_map/ppermute | solution.py:200
  20.0 1.4 %collective-permute-start.6 = (bf16[168,512]{1,0:T(8,128)(2,1)S(1)}, bf16[168,512]{1,0:T(8,128)(2,1)S(1)}, u32[]{:S(2)}, u32[]{:S(2)}) collective-permute-start(bf16[168,512]{1,0:T(8,128)(2,1)S(1)} %collective-permute-done.5.refs_8_), channel_id=1, source_target_pairs={{0,1},{1,0},{2,3},{3,2},{4,5},{5,4},{6,7},{7,6},{8,9},{9,8},{10,11... | collective-permute-start | bytes 516104 | tf_op jit(solution)/shard_map/ppermute | solution.py:200

commit v4 on v0

--- a/solution.py
+++ b/solution.py
@@ -1,7 +1,14 @@
 import jax
 import jax.numpy as jnp
 from jax import lax
+from jax.experimental import pallas as pl
+from jax.experimental.pallas import tpu as pltpu
 from jax.sharding import PartitionSpec as P
+
+F32 = jnp.float32
+BF16 = jnp.bfloat16
+BLOCK = 256
+META_ROWS = 8
 
 
 def margin_terms(arrived, got_codes, risk_weights, correlation, funding_spread):
@@ -26,7 +33,7 @@
     return (margin_now, slot_bar.astype(jnp.bfloat16))
 
 
-def body(
+def exchange_body(
     basis_values, coefficients, trade_cpty, trade_bucket, risk_weights, correlation, funding_spread
 ):
     owners = lax.axis_size("trade")
@@ -60,6 +67,319 @@
     return (margin_now.T, basis_adjoint)
 
 
+def dot(a, b):
+    return jnp.dot(a, b, preferred_element_type=F32)
+
+
+def split(x):
+    hi = x.astype(BF16)
+    return hi, (x - hi.astype(F32)).astype(BF16)
+
+
+def one_hot_t(row, count):
+    ids = lax.broadcasted_iota(jnp.int32, (count, row.shape[1]), 0).astype(F32)
+    return (ids == row).astype(F32).astype(BF16)
+
+
+def pack_kernel(*refs, cpties):
+    sources, out_ref, scratch, sem = refs[:4], refs[4], refs[5:8], refs[8]
+    per, width = sources[3].shape
+    goals = (*scratch, out_ref.at[pl.ds(0, per)])
+    copies = [pltpu.make_async_copy(s, g, sem.at[k]) for k, (s, g) in enumerate(zip(sources, goals))]
+    for copy in copies:
+        copy.start()
+    for copy in copies[:3]:
+        copy.wait()
+    cpty, bucket, spread = (ref[...] for ref in scratch)
+    owner = cpty // cpties
+    high = spread.astype(BF16).astype(F32)
+    middle = (spread - high).astype(BF16).astype(F32)
+    rows = [owner, cpty - owner * cpties, bucket, high, middle, spread - high - middle]
+    out_ref[per:] = jnp.zeros((META_ROWS, width), BF16)
+    for k, row in enumerate(rows):
+        out_ref[per + k : per + k + 1, : row.shape[1]] = row.astype(F32).astype(BF16)
+    copies[3].wait()
+
+
+def cut(start, stop):
+    return [slice(k, min(k + BLOCK, stop)) for k in range(start, stop, BLOCK)]
+
+
+def deltas(basis, coef, rows):
+    return lax.dot_general(
+        basis[...], coef[rows, :], (((1,), (1,)), ((), ())), preferred_element_type=F32
+    ).astype(BF16)
+
+
+def place_shards(coef, sides, both, core, per):
+    spots = [s for s in range(len(both) + 1) if s != EITHER]
+    for s, ref in zip(spots, both):
+        coef[s * per : (s + 1) * per] = ref[:per]
+    for side, ref in enumerate(sides):
+
+        @pl.when(core == side)
+        def _():
+            coef[EITHER * per : (EITHER + 1) * per] = ref[:per]
+
+
+def read_meta(tails, meta, spread, per, cpties):
+    for s, tail in enumerate(tails):
+        meta[:, s * per : (s + 1) * per] = tail[:, :per]
+        spread[:, s * cpties : (s + 1) * cpties] = (
+            tail[3:4, :cpties] + tail[4:5, :cpties] + tail[5:6, :cpties]
+        )
+
+
+def shard_tails(sides, both, core, per):
+    tails = [ref[per : per + META_ROWS].astype(F32) for ref in both]
+    zero, one = (ref[per : per + META_ROWS].astype(F32) for ref in sides)
+    tails.insert(EITHER, jnp.where(core == 0, zero, one))
+    return tails
+
+
+def groups_of(meta, me, core, cpties):
+    offset = meta[0:1, :].astype(jnp.int32) ^ me
+    group = meta[1:2, :]
+    for s in range(1, len(LAYOUT[0])):
+        there = jnp.where(core == 0, LAYOUT[0][s], LAYOUT[1][s])
+        group = group + jnp.where(offset == there, F32(s * cpties), F32(0))
+    return group
+
+
+def pair_factors(table, bucket_t):
+    buckets = bucket_t.shape[0]
+    bucket_hot = bucket_t.T
+    right = [dot(table[k * buckets : (k + 1) * buckets], bucket_t).astype(BF16) for k in range(2)]
+    return jnp.concatenate([bucket_hot, bucket_hot], 1), jnp.concatenate(right, 0)
+
+
+def fill_pairs(left, right, group_col, group, m_hi, m_lo, rows, cols):
+    pair = dot(left[rows], right[:, cols])
+    pair = jnp.where(group_col[rows] == group[:, cols], pair, 0.0)
+    m_hi[rows, cols], m_lo[rows, cols] = split(pair)
+
+
+def column(row, lanes):
+    return jnp.broadcast_to(row, (lanes, row.shape[1])).T[:, :1]
+
+
+def early_kernel(basis_ref, weight_ref, corr_ref, *refs, per, cpties):
+    sides, both = refs[:2], refs[2:5]
+    delta, r_part, table = refs[5:8]
+    basis, coef, weight, corr, meta, spread, m_hi, m_lo, sem = refs[8:]
+    buckets = corr.shape[0]
+    early = delta.shape[1]
+    me, core = lax.axis_index("trade"), lax.axis_index("path")
+    small = [
+        pltpu.make_async_copy(weight_ref, weight, sem.at[0]),
+        pltpu.make_async_copy(corr_ref, corr, sem.at[1]),
+    ]
+    whole = pltpu.make_async_copy(basis_ref, basis, sem.at[2])
+    for copy in (*small, whole):
+        copy.start()
+    read_meta(shard_tails(sides, both, core, per), meta, spread, per, cpties)
+    group = groups_of(meta[:, :early], me, core, cpties)
+    bucket_t = one_hot_t(meta[2:3, :early], buckets)
+    place_shards(coef, sides, both, core, per)
+    for copy in small:
+        copy.wait()
+    weight_col = column(weight[...], buckets)
+    hi, lo = split(corr[...] * weight[...] * weight_col)
+    table[:buckets] = hi
+    table[buckets:] = lo
+    left, right = pair_factors(table, bucket_t)
+    group_col = column(group, buckets)
+    blocks = cut(0, early)
+    for cols in blocks:
+        for rows in blocks:
+            fill_pairs(left, right, group_col, group, m_hi, m_lo, rows, cols)
+    whole.wait()
+    for cols in blocks:
+        delta[:, cols] = deltas(basis, coef, cols)
+    for cols in blocks:
+        r_part[:, cols] = dot(delta[...], m_hi[:, cols]) + dot(delta[...], m_lo[:, cols])
+
+
+def late_kernel(basis_ref, early_delta, r_part, table, *refs, per, cpties):
+    shards = len(LAYOUT[0])
+    sides, both = refs[:2], refs[2 : shards + 1]
+    margin_ref, adj_ref = refs[shards + 1 : shards + 3]
+    basis, coef, meta, spread, delta, m_hi, m_lo, r_all, bar, sem = refs[shards + 3 :]
+    early = early_delta.shape[1]
+    trades = coef.shape[0]
+    groups = spread.shape[1]
+    buckets = table.shape[0] // 2
+    me, core = lax.axis_index("trade"), lax.axis_index("path")
+    whole = pltpu.make_async_copy(basis_ref, basis, sem.at[0])
+    whole.start()
+    read_meta(shard_tails(sides, both, core, per), meta, spread, per, cpties)
+    group = groups_of(meta, me, core, cpties)
+    group_t = one_hot_t(group, groups)
+    group_hot = group_t.T
+    left, right = pair_factors(table, one_hot_t(meta[2:3, :], buckets))
+    group_col = column(group, groups)
+    place_shards(coef, sides, both, core, per)
+    blocks = cut(0, trades)
+
+    def fill(cols):
+        for rows in blocks if cols.start >= early else cut(early, trades):
+            fill_pairs(left, right, group_col, group, m_hi, m_lo, rows, cols)
+
+    whole.wait()
+    delta[:, :early] = early_delta[...]
+    for cols in cut(early, trades):
+        delta[:, cols] = deltas(basis, coef, cols)
+    fill(blocks[0])
+    for k, cols in enumerate(blocks):
+        if k + 1 < len(blocks):
+            fill(blocks[k + 1])
+        if cols.start >= early:
+            r_all[:, cols] = dot(delta[...], m_hi[:, cols]) + dot(delta[...], m_lo[:, cols])
+        else:
+            late = dot(delta[:, early:], m_hi[early:, cols]) + dot(delta[:, early:], m_lo[early:, cols])
+            r_all[:, cols] = r_part[:, cols] + late
+    squares = None
+    for cols in blocks:
+        hi, lo = split(delta[:, cols].astype(F32) * r_all[:, cols])
+        part = dot(hi, group_hot[cols]) + dot(lo, group_hot[cols])
+        squares = part if squares is None else squares + part
+    margin = jnp.sqrt(squares + 1e-06)
+    margin_ref[...] = margin.T[:cpties]
+    hi, lo = split(spread[...] / margin)
+    scale = jnp.concatenate([hi, lo], 1)
+    group_two = jnp.concatenate([group_t, group_t], 0)
+    for cols in blocks:
+        bar[:, cols] = (r_all[:, cols] * dot(scale, group_two[:, cols])).astype(BF16)
+    adj_ref[...] = dot(bar[...], coef[...]).astype(BF16)
+
+
+def swap_cores(x):
+    return lax.ppermute(x, "path", [(0, 1), (1, 0)])
+
+
+def fetch(x, owners, *offsets):
+    pairs = []
+    for core, offset in enumerate(offsets):
+        pairs += [((i ^ offset) * 2 + core, i * 2 + core) for i in range(owners)]
+    return lax.ppermute(x, ("trade", "path"), pairs)
+
+
+LAYOUT = ((0, 4, 2, 1, 5, 3, 6, 7), (0, 2, 4, 1, 3, 5, 7, 6))
+EITHER = 3
+
+
+def hold(x):
+    return pltpu.with_memory_space_constraint(x, pltpu.HBM)
+
+
+def gather_body(
+    basis_values, coefficients, trade_cpty, trade_bucket, risk_weights, correlation, funding_spread
+):
+    owners = lax.axis_size("trade")
+    per = coefficients.shape[0]
+    cpties = funding_spread.shape[0]
+    buckets = risk_weights.shape[0]
+    paths, width = basis_values.shape
+    trades = owners * per
+    vmem = pl.BlockSpec(memory_space=pltpu.VMEM)
+    anywhere = pl.BlockSpec(memory_space=pl.ANY)
+
+    def pack(*refs):
+        pack_kernel(*refs, cpties=cpties)
+
+    payload = pl.pallas_call(
+        pack,
+        out_shape=jax.ShapeDtypeStruct((per + META_ROWS, width), BF16),
+        in_specs=[anywhere] * 4,
+        out_specs=vmem,
+        scratch_shapes=[
+            pltpu.VMEM((1, per), jnp.int32),
+            pltpu.VMEM((1, per), jnp.int32),
+            pltpu.VMEM((1, cpties), F32),
+            pltpu.SemaphoreType.DMA((4,)),
+        ],
+        compiler_params=pltpu.CompilerParams(vmem_limit_bytes=4 << 20),
+    )(
+        hold(trade_cpty.reshape(1, per)),
+        hold(trade_bucket.reshape(1, per)),
+        hold(funding_spread.reshape(1, cpties)),
+        hold(coefficients),
+    )
+    core = lax.axis_index("path")
+    first = fetch(payload, owners, 4, 2)
+    beside = fetch(payload, owners, 0, 1)
+    beside, first = lax.optimization_barrier((beside, first))
+    sent = jnp.where(core == 0, first, beside)
+    second = fetch(sent, owners, 1, 2)
+    first_other = swap_cores(first)
+    _, first_other = lax.optimization_barrier((sent, first_other))
+    opposite = jnp.where(core == 0, first, first_other)
+    third = fetch(opposite, owners, 2, 3)
+    present = (swap_cores(beside), beside, payload, first, first_other)
+    early_trades = trades // 2 // BLOCK * BLOCK
+    groups = owners * cpties
+
+    def early(*refs):
+        early_kernel(*refs, per=per, cpties=cpties)
+
+    state = pl.pallas_call(
+        early,
+        out_shape=[
+            jax.ShapeDtypeStruct((paths, early_trades), BF16),
+            jax.ShapeDtypeStruct((paths, early_trades), F32),
+            jax.ShapeDtypeStruct((2 * buckets, buckets), BF16),
+        ],
+        in_specs=[anywhere] * 3 + [vmem] * len(present),
+        out_specs=[vmem] * 3,
+        scratch_shapes=[
+            pltpu.VMEM((paths, width), BF16),
+            pltpu.VMEM((trades // 2, width), BF16),
+            pltpu.VMEM((1, buckets), F32),
+            pltpu.VMEM((buckets, buckets), F32),
+            pltpu.VMEM((META_ROWS, trades // 2), F32),
+            pltpu.VMEM((1, groups // 2), F32),
+            pltpu.VMEM((early_trades, early_trades), BF16),
+            pltpu.VMEM((early_trades, early_trades), BF16),
+            pltpu.SemaphoreType.DMA((3,)),
+        ],
+        cost_estimate=pl.CostEstimate(flops=2 * 10**9, bytes_accessed=4 * 10**6, transcendentals=0),
+        compiler_params=pltpu.CompilerParams(vmem_limit_bytes=16 << 20),
+    )(
+        hold(basis_values),
+        hold(risk_weights.reshape(1, buckets)),
+        hold(correlation),
+        *present,
+    )
+    second, *state = lax.optimization_barrier((second, *state))
+    shards = present + (second, swap_cores(second), third, swap_cores(third))
+
+    def late(*refs):
+        late_kernel(*refs, per=per, cpties=cpties)
+
+    return pl.pallas_call(
+        late,
+        out_shape=[
+            jax.ShapeDtypeStruct((cpties, paths), F32),
+            jax.ShapeDtypeStruct((paths, width), BF16),
+        ],
+        in_specs=[anywhere] + [vmem] * (len(state) + len(shards)),
+        out_specs=[vmem, vmem],
+        scratch_shapes=[
+            pltpu.VMEM((paths, width), BF16),
+            pltpu.VMEM((trades, width), BF16),
+            pltpu.VMEM((META_ROWS, trades), F32),
+            pltpu.VMEM((1, groups), F32),
+            pltpu.VMEM((paths, trades), BF16),
+            pltpu.VMEM((trades, trades), BF16),
+            pltpu.VMEM((trades, trades), BF16),
+            pltpu.VMEM((paths, trades), F32),
+            pltpu.VMEM((paths, trades), BF16),
+            pltpu.SemaphoreType.DMA((1,)),
+        ],
+        compiler_params=pltpu.CompilerParams(vmem_limit_bytes=36 << 20),
+    )(hold(basis_values), *state, *shards)
+
+
 def solution(mesh):
     placed = (
         P(("date", "path"), None),
@@ -70,8 +390,9 @@
         P(),
         P("trade"),
     )
+    small = mesh.shape["trade"] == 8 and mesh.shape["path"] == 2
     return jax.shard_map(
-        body,
+        gather_body if small else exchange_body,
         mesh=mesh,
         in_specs=placed,
         out_specs=(P("trade", ("date", "path")), P(("date", "path"), None)),

time: 131 us -> 29.7 us (0.23)
  blocking collectives: 71.2 us -> 0 us
  waiting for transfers between devices: 19.8 us -> 6.84 us
  Pallas kernels: 0 us -> 12 us
  local copies, waits for them, and re-layouts: 9.56 us -> 0 us
  matrix products: 8.42 us -> 0 us
  other arithmetic: 6.37 us -> 0.04 us
  starting transfers between devices: 14.3 us -> 9.88 us
    psum x1 -> x0, blocking collectives: 71.2 us -> none  [body(): basis_adjoint = lax.psum(partial_adj, 'trade').astype(jnp.bfloat16)]
    all_to_all x3 -> x0, waiting for transfers between devices: 19.8 us -> none  [the longest x1 9.6 us: body(): lax.all_to_all(slot_bar, 'trade', split_axis=1, concat_axis=1, tiled=True)]
    all_to_all x3 -> x0, starting transfers between devices: 14.3 us -> none  [the longest x1 7.25 us: body(): lax.all_to_all(codes_out, 'trade', split_axis=0, concat_axis=0, tiled=True)]
    pallas_call x0 -> x3, Pallas kernels: none -> 12 us  [the longest x1 8.45 us: gather_body(): pl.pallas_call(late, out_shape=[jax.ShapeDtypeStruct((cpties, paths), F32...]
    ppermute x0 -> x8, starting transfers between devices: none -> 9.88 us  [the longest x4 8.44 us: fetch(): return lax.ppermute(x, ('trade', 'path'), pairs)]
    dot_general x4 -> x0, matrix products: 8.42 us -> none  [the longest x1 5.47 us: margin_terms(): jnp.einsum('pcb,db->pcd', weighted, correlation, precision=lax.Precision....]
    ppermute x0 -> x8, waiting for transfers between devices: none -> 6.84 us  [the longest x4 5.52 us: fetch(): return lax.ppermute(x, ('trade', 'path'), pairs)]
    gather x2 -> x0, local copies, waits for them, and re-layouts: 5.2 us -> none  [the longest x1 4.27 us: margin_terms(): jnp.take(flat_bar, safe_codes, axis=1)]
  transfers between devices with their start and end apart: 3 -> 8, of which waited for: 3 -> 3; matrix products, arithmetic and copies ran while one was open for 4% -> 0% of each run, Pallas kernels for 0% -> 9%
where the time goes in v4:
time: 29.7 us; the launch traced here: 29.5 us
  Pallas kernels  12 us (40%)
  starting transfers between devices  9.88 us (33%)
  waiting for transfers between devices  6.84 us (23%)
  between operations  0.68 us (2%)
    pallas_call x1, Pallas kernels, gather_body(): pl.pallas_call(late, out_shape=[jax.ShapeDtypeStruct((cpties, paths), F32...  8.45 us
    ppermute x4, starting transfers between devices, fetch(): return lax.ppermute(x, ('trade', 'path'), pairs)  8.44 us
    ppermute x4, waiting for transfers between devices, fetch(): return lax.ppermute(x, ('trade', 'path'), pairs)  5.52 us
    pallas_call x1, Pallas kernels, gather_body(): pl.pallas_call(early, out_shape=[jax.ShapeDtypeStruct((paths, early_trade...  2.56 us
    ppermute x4, starting transfers between devices, swap_cores(): return lax.ppermute(x, 'path', [(0, 1), (1, 0)])  1.43 us
    ppermute x4, waiting for transfers between devices, swap_cores(): return lax.ppermute(x, 'path', [(0, 1), (1, 0)])  1.32 us
    pallas_call x1, Pallas kernels, gather_body(): pl.pallas_call(pack, out_shape=jax.ShapeDtypeStruct((per + META_ROWS, wid...  1 us
  transfers between devices with their start and end apart: 8, of which 3 were waited for; matrix products, arithmetic and copies ran while one was open for 0% of the time, Pallas kernels for 9%

profile of v4, /device:TPU:0, one launch (start us, length us, event | category | flops | bytes accessed | tf_op | source)
XLA Modules:
  0.0 29.5 jit_solution(10928282909062041935)
XLA Ops:
  0.6 1.0 %shard_map.86.refs_5_.refs_6_ = bf16[168,512]{1,0:T(8,128)(2,1)S(1)} custom-call(s32[1,160]{1,0:T(1,128)} %bitcast.4, s32[1,160]{1,0:T(1,128)} %bitcast.5, f32[1,16]{1,0:T(1,128)} %bitcast.6, bf16[160,512]{1,0:T(8,128)(2,1)} %refs_3_.1), custom_call_target="tpu_custom_call" | custom-call | tf_op jit(solution)/shard_map/pallas_call | solution.py:290
  1.6 4.1 %collective-permute-start.1 = (bf16[168,512]{1,0:T(8,128)(2,1)S(1)}, bf16[168,512]{1,0:T(8,128)(2,1)S(1)}, u32[]{:S(2)}, u32[]{:S(2)}) collective-permute-start(bf16[168,512]{1,0:T(8,128)(2,1)S(1)} %shard_map.86.refs_5_.refs_6_), channel_id=1, source_target_pairs={{8,0},{10,2},{12,4},{14,6},{0,8},{2,10},{4,12},{6,14},{5,1},{7,3},... | collective-permute-start | bytes 516104 | tf_op jit(solution)/shard_map/ppermute | solution.py:264
  5.7 0.7 %collective-permute-start = (bf16[168,512]{1,0:T(8,128)(2,1)S(1)}, bf16[168,512]{1,0:T(8,128)(2,1)S(1)}, u32[]{:S(2)}, u32[]{:S(2)}) collective-permute-start(bf16[168,512]{1,0:T(8,128)(2,1)S(1)} %shard_map.86.refs_5_.refs_6_), channel_id=1, source_target_pairs={{0,0},{2,2},{4,4},{6,6},{8,8},{10,10},{12,12},{14,14},{3,1},{1,3},... | collective-permute-start | bytes 516104 | tf_op jit(solution)/shard_map/ppermute | solution.py:264
  6.4 3.2 %collective-permute-done.1.refs_6_.refs_7_ = bf16[168,512]{1,0:T(8,128)(2,1)S(1)} collective-permute-done((bf16[168,512]{1,0:T(8,128)(2,1)S(1)}, bf16[168,512]{1,0:T(8,128)(2,1)S(1)}, u32[]{:S(2)}, u32[]{:S(2)}) %collective-permute-start.1) | collective-permute-done | bytes 172064 | tf_op jit(solution)/shard_map/ppermute | solution.py:264
  9.6 0.0 collective-permute-done.refs_4_.refs_5_
  9.6 0.8 %collective-permute-start.3 = (bf16[168,512]{1,0:T(8,128)(2,1)S(1)}, bf16[168,512]{1,0:T(8,128)(2,1)S(1)}, u32[]{:S(2)}, u32[]{:S(2)}) collective-permute-start(bf16[168,512]{1,0:T(8,128)(2,1)S(1)} %collective-permute-done.refs_4_.refs_5_), channel_id=1, source_target_pairs={{0,1},{1,0},{2,3},{3,2},{4,5},{5,4},{6,7},{7,6},{8,9},{9,8},{10,11... | collective-permute-start | bytes 516104 | tf_op jit(solution)/shard_map/ppermute | solution.py:257
  10.4 0.0 collective-permute-start.4
  10.4 1.9 %collective-permute-start.2 = (bf16[168,512]{1,0:T(8,128)(2,1)S(1)}, bf16[168,512]{1,0:T(8,128)(2,1)S(1)}, u32[]{:S(2)}, u32[]{:S(2)}) collective-permute-start(bf16[168,512]{1,0:T(8,128)(2,1)S(1)} %broadcast_select_fusion.1), channel_id=1, source_target_pairs={{2,0},{0,2},{6,4},{4,6},{10,8},{8,10},{14,12},{12,14},{5,1},{7,3},... | collective-permute-start | bytes 516104 | tf_op jit(solution)/shard_map/ppermute | solution.py:264
  12.4 0.0 collective-permute-done.4.refs_7_.refs_8_
  12.4 1.8 %collective-permute-start.6 = (bf16[168,512]{1,0:T(8,128)(2,1)S(1)}, bf16[168,512]{1,0:T(8,128)(2,1)S(1)}, u32[]{:S(2)}, u32[]{:S(2)}) collective-permute-start(bf16[168,512]{1,0:T(8,128)(2,1)S(1)} %broadcast_select_fusion), channel_id=1, source_target_pairs={{4,0},{6,2},{0,4},{2,6},{12,8},{14,10},{8,12},{10,14},{7,1},{5,3},... | collective-permute-start | bytes 516104 | tf_op jit(solution)/shard_map/ppermute | solution.py:264
  14.2 0.0 collective-permute-done.3.refs_3_.refs_4_
  14.2 2.6 %shard_map.87 = (bf16[512,512]{1,0:T(8,128)(2,1)S(1)}, f32[512,512]{1,0:T(8,128)S(1)}, bf16[256,128]{1,0:T(8,128)(2,1)S(1)}) custom-call(bf16[512,512]{1,0:T(8,128)(2,1)} %refs_0_.3, f32[1,128]{1,0:T(1,128)} %bitcast.7, f32[128,128]{1,0:T(8,128)} %refs_2_.1, bf16[168,512]{1,0:T(8,128)(2,1)S(1)} %collective-permute-done.3.refs_3_.refs_4_, ...), custom_call_target="tpu_custom_call" | custom-call | flops 2000000000 | bytes 4000000 | tf_op jit(solution)/shard_map/pallas_call | solution.py:325
  16.7 0.0 collective-permute-done.2.refs_9_
  16.7 0.5 %collective-permute-start.5 = (bf16[168,512]{1,0:T(8,128)(2,1)S(1)}, bf16[168,512]{1,0:T(8,128)(2,1)S(1)}, u32[]{:S(2)}, u32[]{:S(2)}) collective-permute-start(bf16[168,512]{1,0:T(8,128)(2,1)S(1)} %collective-permute-done.2.refs_9_), channel_id=1, source_target_pairs={{0,1},{1,0},{2,3},{3,2},{4,5},{5,4},{6,7},{7,6},{8,9},{9,8},{10,11... | collective-permute-start | bytes 516104 | tf_op jit(solution)/shard_map/ppermute | solution.py:257
  17.3 2.3 %collective-permute-done.6.refs_11_ = bf16[168,512]{1,0:T(8,128)(2,1)S(1)} collective-permute-done((bf16[168,512]{1,0:T(8,128)(2,1)S(1)}, bf16[168,512]{1,0:T(8,128)(2,1)S(1)}, u32[]{:S(2)}, u32[]{:S(2)}) %collective-permute-start.6) | collective-permute-done | bytes 172064 | tf_op jit(solution)/shard_map/ppermute | solution.py:264
  19.6 0.1 collective-permute-start.7
  19.7 0.0 collective-permute-done.5.refs_10_
  19.7 1.3 %collective-permute-done.7.refs_12_ = bf16[168,512]{1,0:T(8,128)(2,1)S(1)} collective-permute-done((bf16[168,512]{1,0:T(8,128)(2,1)S(1)}, bf16[168,512]{1,0:T(8,128)(2,1)S(1)}, u32[]{:S(2)}, u32[]{:S(2)}) %collective-permute-start.7) | collective-permute-done | bytes 172064 | tf_op jit(solution)/shard_map/ppermute | solution.py:257
  21.0 8.5 %shard_map.88 = (f32[16,512]{1,0:T(8,128)}, bf16[512,512]{1,0:T(8,128)(2,1)}) custom-call(bf16[512,512]{1,0:T(8,128)(2,1)} %refs_0_.3, bf16[512,512]{1,0:T(8,128)(2,1)S(1)} %get-tuple-element.18.refs_1_, f32[512,512]{1,0:T(8,128)S(1)} %get-tuple-element.19.refs_2_, bf16[256,128]{1,0:T(8,128)(2,1)S(1)} %get-tuple-element.20.refs_3_, ...), custom_call_target="tpu_custom_call" | custom-call | tf_op jit(solution)/shard_map/pallas_call | solution.py:359
  (2 shorter events, 0.0 us)
Async XLA Ops:
  1.6 8.0 %collective-permute-start.1 = (bf16[168,512]{1,0:T(8,128)(2,1)S(1)}, bf16[168,512]{1,0:T(8,128)(2,1)S(1)}, u32[]{:S(2)}, u32[]{:S(2)}) collective-permute-start(bf16[168,512]{1,0:T(8,128)(2,1)S(1)} %shard_map.86.refs_5_.refs_6_), channel_id=1, source_target_pairs={{8,0},{10,2},{12,4},{14,6},{0,8},{2,10},{4,12},{6,14},{5,1},{7,3},... | collective-permute-start | bytes 516104 | tf_op jit(solution)/shard_map/ppermute | solution.py:264
  5.7 3.9 %collective-permute-start = (bf16[168,512]{1,0:T(8,128)(2,1)S(1)}, bf16[168,512]{1,0:T(8,128)(2,1)S(1)}, u32[]{:S(2)}, u32[]{:S(2)}) collective-permute-start(bf16[168,512]{1,0:T(8,128)(2,1)S(1)} %shard_map.86.refs_5_.refs_6_), channel_id=1, source_target_pairs={{0,0},{2,2},{4,4},{6,6},{8,8},{10,10},{12,12},{14,14},{3,1},{1,3},... | collective-permute-start | bytes 516104 | tf_op jit(solution)/shard_map/ppermute | solution.py:264
  9.6 4.5 %collective-permute-start.3 = (bf16[168,512]{1,0:T(8,128)(2,1)S(1)}, bf16[168,512]{1,0:T(8,128)(2,1)S(1)}, u32[]{:S(2)}, u32[]{:S(2)}) collective-permute-start(bf16[168,512]{1,0:T(8,128)(2,1)S(1)} %collective-permute-done.refs_4_.refs_5_), channel_id=1, source_target_pairs={{0,1},{1,0},{2,3},{3,2},{4,5},{5,4},{6,7},{7,6},{8,9},{9,8},{10,11... | collective-permute-start | bytes 516104 | tf_op jit(solution)/shard_map/ppermute | solution.py:257
  10.4 2.0 %collective-permute-start.4 = (bf16[168,512]{1,0:T(8,128)(2,1)S(1)}, bf16[168,512]{1,0:T(8,128)(2,1)S(1)}, u32[]{:S(2)}, u32[]{:S(2)}) collective-permute-start(bf16[168,512]{1,0:T(8,128)(2,1)S(1)} %collective-permute-done.1.refs_6_.refs_7_), channel_id=1, source_target_pairs={{0,1},{1,0},{2,3},{3,2},{4,5},{5,4},{6,7},{7,6},{8,9},{9,8},{10,11... | collective-permute-start | bytes 516104 | tf_op jit(solution)/shard_map/ppermute | solution.py:257
  10.4 6.3 %collective-permute-start.2 = (bf16[168,512]{1,0:T(8,128)(2,1)S(1)}, bf16[168,512]{1,0:T(8,128)(2,1)S(1)}, u32[]{:S(2)}, u32[]{:S(2)}) collective-permute-start(bf16[168,512]{1,0:T(8,128)(2,1)S(1)} %broadcast_select_fusion.1), channel_id=1, source_target_pairs={{2,0},{0,2},{6,4},{4,6},{10,8},{8,10},{14,12},{12,14},{5,1},{7,3},... | collective-permute-start | bytes 516104 | tf_op jit(solution)/shard_map/ppermute | solution.py:264
  12.4 7.2 %collective-permute-start.6 = (bf16[168,512]{1,0:T(8,128)(2,1)S(1)}, bf16[168,512]{1,0:T(8,128)(2,1)S(1)}, u32[]{:S(2)}, u32[]{:S(2)}) collective-permute-start(bf16[168,512]{1,0:T(8,128)(2,1)S(1)} %broadcast_select_fusion), channel_id=1, source_target_pairs={{4,0},{6,2},{0,4},{2,6},{12,8},{14,10},{8,12},{10,14},{7,1},{5,3},... | collective-permute-start | bytes 516104 | tf_op jit(solution)/shard_map/ppermute | solution.py:264
  16.7 2.9 %collective-permute-start.5 = (bf16[168,512]{1,0:T(8,128)(2,1)S(1)}, bf16[168,512]{1,0:T(8,128)(2,1)S(1)}, u32[]{:S(2)}, u32[]{:S(2)}) collective-permute-start(bf16[168,512]{1,0:T(8,128)(2,1)S(1)} %collective-permute-done.2.refs_9_), channel_id=1, source_target_pairs={{0,1},{1,0},{2,3},{3,2},{4,5},{5,4},{6,7},{7,6},{8,9},{9,8},{10,11... | collective-permute-start | bytes 516104 | tf_op jit(solution)/shard_map/ppermute | solution.py:257
  19.6 1.4 %collective-permute-start.7 = (bf16[168,512]{1,0:T(8,128)(2,1)S(1)}, bf16[168,512]{1,0:T(8,128)(2,1)S(1)}, u32[]{:S(2)}, u32[]{:S(2)}) collective-permute-start(bf16[168,512]{1,0:T(8,128)(2,1)S(1)} %collective-permute-done.6.refs_11_), channel_id=1, source_target_pairs={{0,1},{1,0},{2,3},{3,2},{4,5},{5,4},{6,7},{7,6},{8,9},{9,8},{10,11... | collective-permute-start | bytes 516104 | tf_op jit(solution)/shard_map/ppermute | solution.py:257

commit v5 on v4

--- a/solution.py
+++ b/solution.py
@@ -165,8 +165,8 @@
 
 def early_kernel(basis_ref, weight_ref, corr_ref, *refs, per, cpties):
     sides, both = refs[:2], refs[2:5]
-    delta, r_part, table = refs[5:8]
-    basis, coef, weight, corr, meta, spread, m_hi, m_lo, sem = refs[8:]
+    delta, r_part, table, basis = refs[5:9]
+    coef, weight, corr, meta, spread, m_hi, m_lo, sem = refs[9:]
     buckets = corr.shape[0]
     early = delta.shape[1]
     me, core = lax.axis_index("trade"), lax.axis_index("path")
@@ -200,18 +200,16 @@
         r_part[:, cols] = dot(delta[...], m_hi[:, cols]) + dot(delta[...], m_lo[:, cols])
 
 
-def late_kernel(basis_ref, early_delta, r_part, table, *refs, per, cpties):
+def late_kernel(early_delta, r_part, table, basis, *refs, per, cpties):
     shards = len(LAYOUT[0])
     sides, both = refs[:2], refs[2 : shards + 1]
     margin_ref, adj_ref = refs[shards + 1 : shards + 3]
-    basis, coef, meta, spread, delta, m_hi, m_lo, r_all, bar, sem = refs[shards + 3 :]
+    coef, meta, spread, delta, m_hi, m_lo, r_all, bar = refs[shards + 3 :]
     early = early_delta.shape[1]
     trades = coef.shape[0]
     groups = spread.shape[1]
     buckets = table.shape[0] // 2
     me, core = lax.axis_index("trade"), lax.axis_index("path")
-    whole = pltpu.make_async_copy(basis_ref, basis, sem.at[0])
-    whole.start()
     read_meta(shard_tails(sides, both, core, per), meta, spread, per, cpties)
     group = groups_of(meta, me, core, cpties)
     group_t = one_hot_t(group, groups)
@@ -225,7 +223,6 @@
         for rows in blocks if cols.start >= early else cut(early, trades):
             fill_pairs(left, right, group_col, group, m_hi, m_lo, rows, cols)
 
-    whole.wait()
     delta[:, :early] = early_delta[...]
     for cols in cut(early, trades):
         delta[:, cols] = deltas(basis, coef, cols)
@@ -328,11 +325,11 @@
             jax.ShapeDtypeStruct((paths, early_trades), BF16),
             jax.ShapeDtypeStruct((paths, early_trades), F32),
             jax.ShapeDtypeStruct((2 * buckets, buckets), BF16),
+            jax.ShapeDtypeStruct((paths, width), BF16),
         ],
         in_specs=[anywhere] * 3 + [vmem] * len(present),
-        out_specs=[vmem] * 3,
+        out_specs=[vmem] * 4,
         scratch_shapes=[
-            pltpu.VMEM((paths, width), BF16),
             pltpu.VMEM((trades // 2, width), BF16),
             pltpu.VMEM((1, buckets), F32),
             pltpu.VMEM((buckets, buckets), F32),
@@ -362,10 +359,9 @@
             jax.ShapeDtypeStruct((cpties, paths), F32),
             jax.ShapeDtypeStruct((paths, width), BF16),
         ],
-        in_specs=[anywhere] + [vmem] * (len(state) + len(shards)),
+        in_specs=[vmem] * (len(state) + len(shards)),
         out_specs=[vmem, vmem],
         scratch_shapes=[
-            pltpu.VMEM((paths, width), BF16),
             pltpu.VMEM((trades, width), BF16),
             pltpu.VMEM((META_ROWS, trades), F32),
             pltpu.VMEM((1, groups), F32),
@@ -374,10 +370,9 @@
             pltpu.VMEM((trades, trades), BF16),
             pltpu.VMEM((paths, trades), F32),
             pltpu.VMEM((paths, trades), BF16),
-            pltpu.SemaphoreType.DMA((1,)),
         ],
         compiler_params=pltpu.CompilerParams(vmem_limit_bytes=36 << 20),
-    )(hold(basis_values), *state, *shards)
+    )(*state, *shards)
 
 
 def solution(mesh):

time: 29.7 us -> 28.8 us (0.970)
  Pallas kernels: 12 us -> 11.2 us
    pallas_call x1, Pallas kernels: 8.45 us -> 7.62 us  [gather_body(): pl.pallas_call(late, out_shape=[jax.ShapeDtypeStruct((cpties, paths), F32...]
where the time goes in v5:
time: 28.8 us; the launch traced here: 28.6 us
  Pallas kernels  11.2 us (39%)
  starting transfers between devices  9.86 us (34%)
  waiting for transfers between devices  6.86 us (24%)
  between operations  0.68 us (2%)
    ppermute x4, starting transfers between devices, fetch(): return lax.ppermute(x, ('trade', 'path'), pairs)  8.44 us
    pallas_call x1, Pallas kernels, gather_body(): pl.pallas_call(late, out_shape=[jax.ShapeDtypeStruct((cpties, paths), F32...  7.62 us
    ppermute x4, waiting for transfers between devices, fetch(): return lax.ppermute(x, ('trade', 'path'), pairs)  5.54 us
    pallas_call x1, Pallas kernels, gather_body(): pl.pallas_call(early, out_shape=[jax.ShapeDtypeStruct((paths, early_trade...  2.56 us
    ppermute x4, starting transfers between devices, swap_cores(): return lax.ppermute(x, 'path', [(0, 1), (1, 0)])  1.42 us
    ppermute x4, waiting for transfers between devices, swap_cores(): return lax.ppermute(x, 'path', [(0, 1), (1, 0)])  1.32 us
    pallas_call x1, Pallas kernels, gather_body(): pl.pallas_call(pack, out_shape=jax.ShapeDtypeStruct((per + META_ROWS, wid...  1 us
  transfers between devices with their start and end apart: 8, of which 3 were waited for; matrix products, arithmetic and copies ran while one was open for 0% of the time, Pallas kernels for 9%

profile of v5, /device:TPU:0, one launch (start us, length us, event | category | flops | bytes accessed | tf_op | source)
XLA Modules:
  0.0 28.6 jit_solution(13888074551868795776)
XLA Ops:
  0.6 1.0 %shard_map.86.refs_5_.refs_6_ = bf16[168,512]{1,0:T(8,128)(2,1)S(1)} custom-call(s32[1,160]{1,0:T(1,128)} %bitcast.4, s32[1,160]{1,0:T(1,128)} %bitcast.5, f32[1,16]{1,0:T(1,128)} %bitcast.6, bf16[160,512]{1,0:T(8,128)(2,1)} %refs_3_.1), custom_call_target="tpu_custom_call" | custom-call | tf_op jit(solution)/shard_map/pallas_call | solution.py:287
  1.6 4.1 %collective-permute-start.1 = (bf16[168,512]{1,0:T(8,128)(2,1)S(1)}, bf16[168,512]{1,0:T(8,128)(2,1)S(1)}, u32[]{:S(2)}, u32[]{:S(2)}) collective-permute-start(bf16[168,512]{1,0:T(8,128)(2,1)S(1)} %shard_map.86.refs_5_.refs_6_), channel_id=1, source_target_pairs={{8,0},{10,2},{12,4},{14,6},{0,8},{2,10},{4,12},{6,14},{5,1},{7,3},... | collective-permute-start | bytes 516104 | tf_op jit(solution)/shard_map/ppermute | solution.py:261
  5.7 0.7 %collective-permute-start = (bf16[168,512]{1,0:T(8,128)(2,1)S(1)}, bf16[168,512]{1,0:T(8,128)(2,1)S(1)}, u32[]{:S(2)}, u32[]{:S(2)}) collective-permute-start(bf16[168,512]{1,0:T(8,128)(2,1)S(1)} %shard_map.86.refs_5_.refs_6_), channel_id=1, source_target_pairs={{0,0},{2,2},{4,4},{6,6},{8,8},{10,10},{12,12},{14,14},{3,1},{1,3},... | collective-permute-start | bytes 516104 | tf_op jit(solution)/shard_map/ppermute | solution.py:261
  6.4 3.2 %collective-permute-done.1.refs_6_.refs_7_ = bf16[168,512]{1,0:T(8,128)(2,1)S(1)} collective-permute-done((bf16[168,512]{1,0:T(8,128)(2,1)S(1)}, bf16[168,512]{1,0:T(8,128)(2,1)S(1)}, u32[]{:S(2)}, u32[]{:S(2)}) %collective-permute-start.1) | collective-permute-done | bytes 172064 | tf_op jit(solution)/shard_map/ppermute | solution.py:261
  9.6 0.0 collective-permute-done.refs_4_.refs_5_
  9.6 0.8 %collective-permute-start.3 = (bf16[168,512]{1,0:T(8,128)(2,1)S(1)}, bf16[168,512]{1,0:T(8,128)(2,1)S(1)}, u32[]{:S(2)}, u32[]{:S(2)}) collective-permute-start(bf16[168,512]{1,0:T(8,128)(2,1)S(1)} %collective-permute-done.refs_4_.refs_5_), channel_id=1, source_target_pairs={{0,1},{1,0},{2,3},{3,2},{4,5},{5,4},{6,7},{7,6},{8,9},{9,8},{10,11... | collective-permute-start | bytes 516104 | tf_op jit(solution)/shard_map/ppermute | solution.py:254
  10.4 0.0 collective-permute-start.4
  10.4 1.9 %collective-permute-start.2 = (bf16[168,512]{1,0:T(8,128)(2,1)S(1)}, bf16[168,512]{1,0:T(8,128)(2,1)S(1)}, u32[]{:S(2)}, u32[]{:S(2)}) collective-permute-start(bf16[168,512]{1,0:T(8,128)(2,1)S(1)} %broadcast_select_fusion.1), channel_id=1, source_target_pairs={{2,0},{0,2},{6,4},{4,6},{10,8},{8,10},{14,12},{12,14},{5,1},{7,3},... | collective-permute-start | bytes 516104 | tf_op jit(solution)/shard_map/ppermute | solution.py:261
  12.4 0.0 collective-permute-done.4.refs_7_.refs_8_
  12.4 1.8 %collective-permute-start.6 = (bf16[168,512]{1,0:T(8,128)(2,1)S(1)}, bf16[168,512]{1,0:T(8,128)(2,1)S(1)}, u32[]{:S(2)}, u32[]{:S(2)}) collective-permute-start(bf16[168,512]{1,0:T(8,128)(2,1)S(1)} %broadcast_select_fusion), channel_id=1, source_target_pairs={{4,0},{6,2},{0,4},{2,6},{12,8},{14,10},{8,12},{10,14},{7,1},{5,3},... | collective-permute-start | bytes 516104 | tf_op jit(solution)/shard_map/ppermute | solution.py:261
  14.2 0.0 collective-permute-done.3.refs_3_.refs_4_
  14.2 2.6 %shard_map.87 = (bf16[512,512]{1,0:T(8,128)(2,1)S(1)}, f32[512,512]{1,0:T(8,128)S(1)}, bf16[256,128]{1,0:T(8,128)(2,1)S(1)}, bf16[512,512]{1,0:T(8,128)(2,1)S(1)}) custom-call(bf16[512,512]{1,0:T(8,128)(2,1)} %refs_0_.1, f32[1,128]{1,0:T(1,128)} %bitcast.7, f32[128,128]{1,0:T(8,128)} %refs_2_.1, bf16[168,512]{1,0:T(8,128)(2,1)S(1)} %collective-permute-done.3.refs_3_.refs_4_, ...), custom_call_target="tpu_custom_call" | custom-call | flops 2000000000 | bytes 4000000 | tf_op jit(solution)/shard_map/pallas_call | solution.py:322
  16.7 0.0 collective-permute-done.2.refs_9_
  16.7 0.5 %collective-permute-start.5 = (bf16[168,512]{1,0:T(8,128)(2,1)S(1)}, bf16[168,512]{1,0:T(8,128)(2,1)S(1)}, u32[]{:S(2)}, u32[]{:S(2)}) collective-permute-start(bf16[168,512]{1,0:T(8,128)(2,1)S(1)} %collective-permute-done.2.refs_9_), channel_id=1, source_target_pairs={{0,1},{1,0},{2,3},{3,2},{4,5},{5,4},{6,7},{7,6},{8,9},{9,8},{10,11... | collective-permute-start | bytes 516104 | tf_op jit(solution)/shard_map/ppermute | solution.py:254
  17.3 2.3 %collective-permute-done.6.refs_11_ = bf16[168,512]{1,0:T(8,128)(2,1)S(1)} collective-permute-done((bf16[168,512]{1,0:T(8,128)(2,1)S(1)}, bf16[168,512]{1,0:T(8,128)(2,1)S(1)}, u32[]{:S(2)}, u32[]{:S(2)}) %collective-permute-start.6) | collective-permute-done | bytes 172064 | tf_op jit(solution)/shard_map/ppermute | solution.py:261
  19.6 0.1 collective-permute-start.7
  19.7 0.0 collective-permute-done.5.refs_10_
  19.7 1.3 %collective-permute-done.7.refs_12_ = bf16[168,512]{1,0:T(8,128)(2,1)S(1)} collective-permute-done((bf16[168,512]{1,0:T(8,128)(2,1)S(1)}, bf16[168,512]{1,0:T(8,128)(2,1)S(1)}, u32[]{:S(2)}, u32[]{:S(2)}) %collective-permute-start.7) | collective-permute-done | bytes 172064 | tf_op jit(solution)/shard_map/ppermute | solution.py:254
  21.0 7.6 %shard_map.88 = (f32[16,512]{1,0:T(8,128)}, bf16[512,512]{1,0:T(8,128)(2,1)}) custom-call(bf16[512,512]{1,0:T(8,128)(2,1)S(1)} %get-tuple-element.21.refs_0_, f32[512,512]{1,0:T(8,128)S(1)} %get-tuple-element.22.refs_1_, bf16[256,128]{1,0:T(8,128)(2,1)S(1)} %get-tuple-element.23.refs_2_, bf16[512,512]{1,0:T(8,128)(2,1)S(1)} %get-tuple-element.24.refs_3_, ...), custom_call_target="tpu_custom_call" | custom-call | tf_op jit(solution)/shard_map/pallas_call | solution.py:356
  (2 shorter events, 0.0 us)
Async XLA Ops:
  1.6 8.0 %collective-permute-start.1 = (bf16[168,512]{1,0:T(8,128)(2,1)S(1)}, bf16[168,512]{1,0:T(8,128)(2,1)S(1)}, u32[]{:S(2)}, u32[]{:S(2)}) collective-permute-start(bf16[168,512]{1,0:T(8,128)(2,1)S(1)} %shard_map.86.refs_5_.refs_6_), channel_id=1, source_target_pairs={{8,0},{10,2},{12,4},{14,6},{0,8},{2,10},{4,12},{6,14},{5,1},{7,3},... | collective-permute-start | bytes 516104 | tf_op jit(solution)/shard_map/ppermute | solution.py:261
  5.7 3.9 %collective-permute-start = (bf16[168,512]{1,0:T(8,128)(2,1)S(1)}, bf16[168,512]{1,0:T(8,128)(2,1)S(1)}, u32[]{:S(2)}, u32[]{:S(2)}) collective-permute-start(bf16[168,512]{1,0:T(8,128)(2,1)S(1)} %shard_map.86.refs_5_.refs_6_), channel_id=1, source_target_pairs={{0,0},{2,2},{4,4},{6,6},{8,8},{10,10},{12,12},{14,14},{3,1},{1,3},... | collective-permute-start | bytes 516104 | tf_op jit(solution)/shard_map/ppermute | solution.py:261
  9.6 4.5 %collective-permute-start.3 = (bf16[168,512]{1,0:T(8,128)(2,1)S(1)}, bf16[168,512]{1,0:T(8,128)(2,1)S(1)}, u32[]{:S(2)}, u32[]{:S(2)}) collective-permute-start(bf16[168,512]{1,0:T(8,128)(2,1)S(1)} %collective-permute-done.refs_4_.refs_5_), channel_id=1, source_target_pairs={{0,1},{1,0},{2,3},{3,2},{4,5},{5,4},{6,7},{7,6},{8,9},{9,8},{10,11... | collective-permute-start | bytes 516104 | tf_op jit(solution)/shard_map/ppermute | solution.py:254
  10.4 2.0 %collective-permute-start.4 = (bf16[168,512]{1,0:T(8,128)(2,1)S(1)}, bf16[168,512]{1,0:T(8,128)(2,1)S(1)}, u32[]{:S(2)}, u32[]{:S(2)}) collective-permute-start(bf16[168,512]{1,0:T(8,128)(2,1)S(1)} %collective-permute-done.1.refs_6_.refs_7_), channel_id=1, source_target_pairs={{0,1},{1,0},{2,3},{3,2},{4,5},{5,4},{6,7},{7,6},{8,9},{9,8},{10,11... | collective-permute-start | bytes 516104 | tf_op jit(solution)/shard_map/ppermute | solution.py:254
  10.4 6.3 %collective-permute-start.2 = (bf16[168,512]{1,0:T(8,128)(2,1)S(1)}, bf16[168,512]{1,0:T(8,128)(2,1)S(1)}, u32[]{:S(2)}, u32[]{:S(2)}) collective-permute-start(bf16[168,512]{1,0:T(8,128)(2,1)S(1)} %broadcast_select_fusion.1), channel_id=1, source_target_pairs={{2,0},{0,2},{6,4},{4,6},{10,8},{8,10},{14,12},{12,14},{5,1},{7,3},... | collective-permute-start | bytes 516104 | tf_op jit(solution)/shard_map/ppermute | solution.py:261
  12.4 7.2 %collective-permute-start.6 = (bf16[168,512]{1,0:T(8,128)(2,1)S(1)}, bf16[168,512]{1,0:T(8,128)(2,1)S(1)}, u32[]{:S(2)}, u32[]{:S(2)}) collective-permute-start(bf16[168,512]{1,0:T(8,128)(2,1)S(1)} %broadcast_select_fusion), channel_id=1, source_target_pairs={{4,0},{6,2},{0,4},{2,6},{12,8},{14,10},{8,12},{10,14},{7,1},{5,3},... | collective-permute-start | bytes 516104 | tf_op jit(solution)/shard_map/ppermute | solution.py:261
  16.7 3.0 %collective-permute-start.5 = (bf16[168,512]{1,0:T(8,128)(2,1)S(1)}, bf16[168,512]{1,0:T(8,128)(2,1)S(1)}, u32[]{:S(2)}, u32[]{:S(2)}) collective-permute-start(bf16[168,512]{1,0:T(8,128)(2,1)S(1)} %collective-permute-done.2.refs_9_), channel_id=1, source_target_pairs={{0,1},{1,0},{2,3},{3,2},{4,5},{5,4},{6,7},{7,6},{8,9},{9,8},{10,11... | collective-permute-start | bytes 516104 | tf_op jit(solution)/shard_map/ppermute | solution.py:254
  19.6 1.4 %collective-permute-start.7 = (bf16[168,512]{1,0:T(8,128)(2,1)S(1)}, bf16[168,512]{1,0:T(8,128)(2,1)S(1)}, u32[]{:S(2)}, u32[]{:S(2)}) collective-permute-start(bf16[168,512]{1,0:T(8,128)(2,1)S(1)} %collective-permute-done.6.refs_11_), channel_id=1, source_target_pairs={{0,1},{1,0},{2,3},{3,2},{4,5},{5,4},{6,7},{7,6},{8,9},{9,8},{10,11... | collective-permute-start | bytes 516104 | tf_op jit(solution)/shard_map/ppermute | solution.py:254

commit v6 on v5

--- a/solution.py
+++ b/solution.py
@@ -111,10 +111,11 @@
     ).astype(BF16)
 
 
-def place_shards(coef, sides, both, core, per):
+def place_shards(coef, sides, both, core, per, start=0):
     spots = [s for s in range(len(both) + 1) if s != EITHER]
     for s, ref in zip(spots, both):
-        coef[s * per : (s + 1) * per] = ref[:per]
+        if s >= start:
+            coef[s * per : (s + 1) * per] = ref[:per]
     for side, ref in enumerate(sides):
 
         @pl.when(core == side)
@@ -161,6 +162,25 @@
 
 def column(row, lanes):
     return jnp.broadcast_to(row, (lanes, row.shape[1])).T[:, :1]
+
+
+def advance(basis, coef, delta, m_hi, m_lo, factors, group_col, group, done, upto, prior, r_out):
+    left, right = factors
+    blocks = cut(0, upto)
+
+    def fill(cols):
+        for rows in blocks if cols.start >= done else cut(done, upto):
+            fill_pairs(left, right, group_col, group, m_hi, m_lo, rows, cols)
+
+    for cols in cut(done, upto):
+        delta[:, cols] = deltas(basis, coef, cols)
+    fill(blocks[0])
+    for k, cols in enumerate(blocks):
+        if k + 1 < len(blocks):
+            fill(blocks[k + 1])
+        inner = slice(0 if cols.start >= done else done, upto)
+        r = dot(delta[:, inner], m_hi[inner, cols]) + dot(delta[:, inner], m_lo[inner, cols])
+        r_out[:, cols] = r if cols.start >= done else prior[:, cols] + r
 
 
 def early_kernel(basis_ref, weight_ref, corr_ref, *refs, per, cpties):
@@ -187,26 +207,36 @@
     hi, lo = split(corr[...] * weight[...] * weight_col)
     table[:buckets] = hi
     table[buckets:] = lo
-    left, right = pair_factors(table, bucket_t)
-    group_col = column(group, buckets)
-    blocks = cut(0, early)
-    for cols in blocks:
-        for rows in blocks:
-            fill_pairs(left, right, group_col, group, m_hi, m_lo, rows, cols)
+    factors = pair_factors(table, bucket_t)
     whole.wait()
-    for cols in blocks:
-        delta[:, cols] = deltas(basis, coef, cols)
-    for cols in blocks:
-        r_part[:, cols] = dot(delta[...], m_hi[:, cols]) + dot(delta[...], m_lo[:, cols])
-
-
-def late_kernel(early_delta, r_part, table, basis, *refs, per, cpties):
+    advance(
+        basis, coef, delta, m_hi, m_lo, factors, column(group, buckets), group, 0, early, None, r_part
+    )
+
+
+def middle_kernel(prior_delta, prior, table, basis, *refs, per, cpties):
+    sides, both = refs[:2], refs[2:6]
+    delta, r_part = refs[6:8]
+    coef, meta, spread, m_hi, m_lo = refs[8:]
+    done, upto = prior_delta.shape[1], delta.shape[1]
+    buckets = table.shape[0] // 2
+    me, core = lax.axis_index("trade"), lax.axis_index("path")
+    read_meta(shard_tails(sides, both, core, per), meta, spread, per, cpties)
+    group = groups_of(meta[:, :upto], me, core, cpties)
+    factors = pair_factors(table, one_hot_t(meta[2:3, :upto], buckets))
+    place_shards(coef, sides, both, core, per, EITHER)
+    delta[:, :done] = prior_delta[...]
+    advance(
+        basis, coef, delta, m_hi, m_lo, factors, column(group, buckets), group, done, upto, prior, r_part
+    )
+
+
+def late_kernel(prior_delta, prior, table, basis, *refs, per, cpties):
     shards = len(LAYOUT[0])
     sides, both = refs[:2], refs[2 : shards + 1]
     margin_ref, adj_ref = refs[shards + 1 : shards + 3]
     coef, meta, spread, delta, m_hi, m_lo, r_all, bar = refs[shards + 3 :]
-    early = early_delta.shape[1]
-    trades = coef.shape[0]
+    done, trades = prior_delta.shape[1], coef.shape[0]
     groups = spread.shape[1]
     buckets = table.shape[0] // 2
     me, core = lax.axis_index("trade"), lax.axis_index("path")
@@ -214,27 +244,13 @@
     group = groups_of(meta, me, core, cpties)
     group_t = one_hot_t(group, groups)
     group_hot = group_t.T
-    left, right = pair_factors(table, one_hot_t(meta[2:3, :], buckets))
-    group_col = column(group, groups)
+    factors = pair_factors(table, one_hot_t(meta[2:3, :], buckets))
     place_shards(coef, sides, both, core, per)
+    delta[:, :done] = prior_delta[...]
+    advance(
+        basis, coef, delta, m_hi, m_lo, factors, column(group, groups), group, done, trades, prior, r_all
+    )
     blocks = cut(0, trades)
-
-    def fill(cols):
-        for rows in blocks if cols.start >= early else cut(early, trades):
-            fill_pairs(left, right, group_col, group, m_hi, m_lo, rows, cols)
-
-    delta[:, :early] = early_delta[...]
-    for cols in cut(early, trades):
-        delta[:, cols] = deltas(basis, coef, cols)
-    fill(blocks[0])
-    for k, cols in enumerate(blocks):
-        if k + 1 < len(blocks):
-            fill(blocks[k + 1])
-        if cols.start >= early:
-            r_all[:, cols] = dot(delta[...], m_hi[:, cols]) + dot(delta[...], m_lo[:, cols])
-        else:
-            late = dot(delta[:, early:], m_hi[early:, cols]) + dot(delta[:, early:], m_lo[early:, cols])
-            r_all[:, cols] = r_part[:, cols] + late
     squares = None
     for cols in blocks:
         hi, lo = split(delta[:, cols].astype(F32) * r_all[:, cols])
@@ -305,7 +321,7 @@
     core = lax.axis_index("path")
     first = fetch(payload, owners, 4, 2)
     beside = fetch(payload, owners, 0, 1)
-    beside, first = lax.optimization_barrier((beside, first))
+    first, beside = lax.optimization_barrier((first, beside))
     sent = jnp.where(core == 0, first, beside)
     second = fetch(sent, owners, 1, 2)
     first_other = swap_cores(first)
@@ -348,7 +364,34 @@
         *present,
     )
     second, *state = lax.optimization_barrier((second, *state))
-    shards = present + (second, swap_cores(second), third, swap_cores(third))
+    second_other = swap_cores(second)
+    middle_trades = 5 * per // BLOCK * BLOCK
+
+    def middle(*refs):
+        middle_kernel(*refs, per=per, cpties=cpties)
+
+    table, basis = state[2:]
+    state = pl.pallas_call(
+        middle,
+        out_shape=[
+            jax.ShapeDtypeStruct((paths, middle_trades), BF16),
+            jax.ShapeDtypeStruct((paths, middle_trades), F32),
+        ],
+        in_specs=[vmem] * (len(state) + len(present) + 1),
+        out_specs=[vmem] * 2,
+        scratch_shapes=[
+            pltpu.VMEM((5 * per, width), BF16),
+            pltpu.VMEM((META_ROWS, 5 * per), F32),
+            pltpu.VMEM((1, 5 * cpties), F32),
+            pltpu.VMEM((middle_trades, middle_trades), BF16),
+            pltpu.VMEM((middle_trades, middle_trades), BF16),
+        ],
+        cost_estimate=pl.CostEstimate(flops=1000, bytes_accessed=1000, transcendentals=0),
+        compiler_params=pltpu.CompilerParams(vmem_limit_bytes=16 << 20),
+    )(*state, *present, second)
+    third, *state = lax.optimization_barrier((third, *state))
+    state = (*state, table, basis)
+    shards = present + (second, second_other, third, swap_cores(third))
 
     def late(*refs):
         late_kernel(*refs, per=per, cpties=cpties)

time: 28.8 us -> 28.2 us (0.979)
  the two profiles are of different devices: /device:TPU:0 before, /device:TPU:27 now
where the time goes in v6:
time: 28.2 us; the launch traced here: 28 us
  Pallas kernels  12.3 us (44%)
  starting transfers between devices  7.96 us (28%)
  waiting for transfers between devices  7.02 us (25%)
  between operations  0.7 us (2%)
    pallas_call x1, Pallas kernels, gather_body(): pl.pallas_call(late, out_shape=[jax.ShapeDtypeStruct((cpties, paths), F32...  6.56 us
    ppermute x4, starting transfers between devices, swap_cores(): return lax.ppermute(x, 'path', [(0, 1), (1, 0)])  4.95 us
    ppermute x4, waiting for transfers between devices, fetch(): return lax.ppermute(x, ('trade', 'path'), pairs)  4.7 us
    ppermute x4, starting transfers between devices, fetch(): return lax.ppermute(x, ('trade', 'path'), pairs)  3.02 us
    pallas_call x1, Pallas kernels, gather_body(): pl.pallas_call(early, out_shape=[jax.ShapeDtypeStruct((paths, early_trade...  2.58 us
    ppermute x4, waiting for transfers between devices, swap_cores(): return lax.ppermute(x, 'path', [(0, 1), (1, 0)])  2.32 us
    pallas_call x1, Pallas kernels, gather_body(): pl.pallas_call(middle, out_shape=[jax.ShapeDtypeStruct((paths, middle_tra...  2.16 us
    pallas_call x1, Pallas kernels, gather_body(): pl.pallas_call(pack, out_shape=jax.ShapeDtypeStruct((per + META_ROWS, wid...  1 us
  transfers between devices with their start and end apart: 8, of which 5 were waited for; matrix products, arithmetic and copies ran while one was open for 0% of the time, Pallas kernels for 17%

profile of v6, /device:TPU:27, one launch (start us, length us, event | category | flops | bytes accessed | tf_op | source)
XLA Modules:
  0.0 28.0 jit_solution(5603195883013965021)
XLA Ops:
  0.6 1.0 %shard_map.86.refs_5_.refs_6_ = bf16[168,512]{1,0:T(8,128)(2,1)S(1)} custom-call(s32[1,160]{1,0:T(1,128)} %bitcast.4, s32[1,160]{1,0:T(1,128)} %bitcast.5, f32[1,16]{1,0:T(1,128)} %bitcast.6, bf16[160,512]{1,0:T(8,128)(2,1)} %refs_3_.1), custom_call_target="tpu_custom_call" | custom-call | tf_op jit(solution)/shard_map/pallas_call | solution.py:303
  1.6 0.2 collective-permute-start
  1.9 2.2 %collective-permute-start.1 = (bf16[168,512]{1,0:T(8,128)(2,1)S(1)}, bf16[168,512]{1,0:T(8,128)(2,1)S(1)}, u32[]{:S(2)}, u32[]{:S(2)}) collective-permute-start(bf16[168,512]{1,0:T(8,128)(2,1)S(1)} %shard_map.86.refs_5_.refs_6_), channel_id=1, source_target_pairs={{0,0},{2,2},{4,4},{6,6},{8,8},{10,10},{12,12},{14,14},{3,1},{1,3},... | collective-permute-start | bytes 516104 | tf_op jit(solution)/shard_map/ppermute | solution.py:277
  4.0 1.9 %collective-permute-done.refs_6_.refs_7_ = bf16[168,512]{1,0:T(8,128)(2,1)S(1)} collective-permute-done((bf16[168,512]{1,0:T(8,128)(2,1)S(1)}, bf16[168,512]{1,0:T(8,128)(2,1)S(1)}, u32[]{:S(2)}, u32[]{:S(2)}) %collective-permute-start) | collective-permute-done | bytes 172064 | tf_op jit(solution)/shard_map/ppermute | solution.py:277
  6.0 2.3 %collective-permute-done.1.refs_4_.refs_5_ = bf16[168,512]{1,0:T(8,128)(2,1)S(1)} collective-permute-done((bf16[168,512]{1,0:T(8,128)(2,1)S(1)}, bf16[168,512]{1,0:T(8,128)(2,1)S(1)}, u32[]{:S(2)}, u32[]{:S(2)}) %collective-permute-start.1) | collective-permute-done | bytes 172064 | tf_op jit(solution)/shard_map/ppermute | solution.py:277
  8.3 2.1 %collective-permute-start.2 = (bf16[168,512]{1,0:T(8,128)(2,1)S(1)}, bf16[168,512]{1,0:T(8,128)(2,1)S(1)}, u32[]{:S(2)}, u32[]{:S(2)}) collective-permute-start(bf16[168,512]{1,0:T(8,128)(2,1)S(1)} %collective-permute-done.refs_6_.refs_7_), channel_id=1, source_target_pairs={{0,1},{1,0},{2,3},{3,2},{4,5},{5,4},{6,7},{7,6},{8,9},{9,8},{10,11... | collective-permute-start | bytes 516104 | tf_op jit(solution)/shard_map/ppermute | solution.py:270
  10.4 0.0 collective-permute-start.5
  10.4 0.1 collective-permute-start.4
  10.5 0.9 %collective-permute-done.2.refs_7_.refs_8_ = bf16[168,512]{1,0:T(8,128)(2,1)S(1)} collective-permute-done((bf16[168,512]{1,0:T(8,128)(2,1)S(1)}, bf16[168,512]{1,0:T(8,128)(2,1)S(1)}, u32[]{:S(2)}, u32[]{:S(2)}) %collective-permute-start.2) | collective-permute-done | bytes 172064 | tf_op jit(solution)/shard_map/ppermute | solution.py:270
  11.5 0.6 %collective-permute-start.3 = (bf16[168,512]{1,0:T(8,128)(2,1)S(1)}, bf16[168,512]{1,0:T(8,128)(2,1)S(1)}, u32[]{:S(2)}, u32[]{:S(2)}) collective-permute-start(bf16[168,512]{1,0:T(8,128)(2,1)S(1)} %broadcast_select_fusion), channel_id=1, source_target_pairs={{4,0},{6,2},{0,4},{2,6},{12,8},{14,10},{8,12},{10,14},{7,1},{5,3},... | collective-permute-start | bytes 516104 | tf_op jit(solution)/shard_map/ppermute | solution.py:277
  12.0 0.0 collective-permute-done.5.refs_3_.refs_4_
  12.0 2.6 %shard_map.87 = (bf16[512,512]{1,0:T(8,128)(2,1)S(1)}, f32[512,512]{1,0:T(8,128)S(1)}, bf16[256,128]{1,0:T(8,128)(2,1)S(1)}, bf16[512,512]{1,0:T(8,128)(2,1)S(1)}) custom-call(bf16[512,512]{1,0:T(8,128)(2,1)} %refs_0_.1, f32[1,128]{1,0:T(1,128)} %bitcast.7, f32[128,128]{1,0:T(8,128)} %refs_2_.1, bf16[168,512]{1,0:T(8,128)(2,1)S(1)} %collective-permute-done.5.refs_3_.refs_4_, ...), custom_call_target="tpu_custom_call" | custom-call | flops 2000000000 | bytes 4000000 | tf_op jit(solution)/shard_map/pallas_call | solution.py:338
  14.6 0.4 %collective-permute-done.4.refs_9_ = bf16[168,512]{1,0:T(8,128)(2,1)S(1)} collective-permute-done((bf16[168,512]{1,0:T(8,128)(2,1)S(1)}, bf16[168,512]{1,0:T(8,128)(2,1)S(1)}, u32[]{:S(2)}, u32[]{:S(2)}) %collective-permute-start.4) | collective-permute-done | bytes 172064 | tf_op jit(solution)/shard_map/ppermute | solution.py:277
  15.1 2.8 %collective-permute-start.6 = (bf16[168,512]{1,0:T(8,128)(2,1)S(1)}, bf16[168,512]{1,0:T(8,128)(2,1)S(1)}, u32[]{:S(2)}, u32[]{:S(2)}) collective-permute-start(bf16[168,512]{1,0:T(8,128)(2,1)S(1)} %collective-permute-done.4.refs_9_), channel_id=1, source_target_pairs={{0,1},{1,0},{2,3},{3,2},{4,5},{5,4},{6,7},{7,6},{8,9},{9,8},{10,11... | collective-permute-start | bytes 516104 | tf_op jit(solution)/shard_map/ppermute | solution.py:270
  17.8 2.2 %shard_map.88 = (bf16[512,768]{1,0:T(8,128)(2,1)S(1)}, f32[512,768]{1,0:T(8,128)S(1)}) custom-call(bf16[512,512]{1,0:T(8,128)(2,1)S(1)} %get-tuple-element.26.refs_0_, f32[512,512]{1,0:T(8,128)S(1)} %get-tuple-element.27.refs_1_, bf16[256,128]{1,0:T(8,128)(2,1)S(1)} %get-tuple-element.28.refs_2_, bf16[512,512]{1,0:T(8,128)(2,1)S(1)} %get-tuple-element.29.refs_3_, ...), custom_call_target="tpu_custom_call" | custom-call | flops 1000 | bytes 1000 | tf_op jit(solution)/shard_map/pallas_call | solution.py:374
  20.0 0.0 collective-permute-done.3.refs_11_
  20.0 0.1 collective-permute-start.7
  20.1 0.0 collective-permute-done.6.refs_10_
  20.1 1.4 %collective-permute-done.7.refs_12_ = bf16[168,512]{1,0:T(8,128)(2,1)S(1)} collective-permute-done((bf16[168,512]{1,0:T(8,128)(2,1)S(1)}, bf16[168,512]{1,0:T(8,128)(2,1)S(1)}, u32[]{:S(2)}, u32[]{:S(2)}) %collective-permute-start.7) | collective-permute-done | bytes 172064 | tf_op jit(solution)/shard_map/ppermute | solution.py:270
  21.5 6.6 %shard_map.89 = (f32[16,512]{1,0:T(8,128)}, bf16[512,512]{1,0:T(8,128)(2,1)}) custom-call(bf16[512,768]{1,0:T(8,128)(2,1)S(1)} %get-tuple-element.33.refs_0_, f32[512,768]{1,0:T(8,128)S(1)} %get-tuple-element.34.refs_1_, bf16[256,128]{1,0:T(8,128)(2,1)S(1)} %get-tuple-element.28.refs_2_, bf16[512,512]{1,0:T(8,128)(2,1)S(1)} %get-tuple-element.29.refs_3_, ...), custom_call_target="tpu_custom_call" | custom-call | tf_op jit(solution)/shard_map/pallas_call | solution.py:399
  (2 shorter events, 0.0 us)
Async XLA Ops:
  1.6 4.3 %collective-permute-start = (bf16[168,512]{1,0:T(8,128)(2,1)S(1)}, bf16[168,512]{1,0:T(8,128)(2,1)S(1)}, u32[]{:S(2)}, u32[]{:S(2)}) collective-permute-start(bf16[168,512]{1,0:T(8,128)(2,1)S(1)} %shard_map.86.refs_5_.refs_6_), channel_id=1, source_target_pairs={{8,0},{10,2},{12,4},{14,6},{0,8},{2,10},{4,12},{6,14},{5,1},{7,3},... | collective-permute-start | bytes 516104 | tf_op jit(solution)/shard_map/ppermute | solution.py:277
  1.9 6.4 %collective-permute-start.1 = (bf16[168,512]{1,0:T(8,128)(2,1)S(1)}, bf16[168,512]{1,0:T(8,128)(2,1)S(1)}, u32[]{:S(2)}, u32[]{:S(2)}) collective-permute-start(bf16[168,512]{1,0:T(8,128)(2,1)S(1)} %shard_map.86.refs_5_.refs_6_), channel_id=1, source_target_pairs={{0,0},{2,2},{4,4},{6,6},{8,8},{10,10},{12,12},{14,14},{3,1},{1,3},... | collective-permute-start | bytes 516104 | tf_op jit(solution)/shard_map/ppermute | solution.py:277
  8.3 3.2 %collective-permute-start.2 = (bf16[168,512]{1,0:T(8,128)(2,1)S(1)}, bf16[168,512]{1,0:T(8,128)(2,1)S(1)}, u32[]{:S(2)}, u32[]{:S(2)}) collective-permute-start(bf16[168,512]{1,0:T(8,128)(2,1)S(1)} %collective-permute-done.refs_6_.refs_7_), channel_id=1, source_target_pairs={{0,1},{1,0},{2,3},{3,2},{4,5},{5,4},{6,7},{7,6},{8,9},{9,8},{10,11... | collective-permute-start | bytes 516104 | tf_op jit(solution)/shard_map/ppermute | solution.py:270
  10.4 1.6 %collective-permute-start.5 = (bf16[168,512]{1,0:T(8,128)(2,1)S(1)}, bf16[168,512]{1,0:T(8,128)(2,1)S(1)}, u32[]{:S(2)}, u32[]{:S(2)}) collective-permute-start(bf16[168,512]{1,0:T(8,128)(2,1)S(1)} %collective-permute-done.1.refs_4_.refs_5_), channel_id=1, source_target_pairs={{0,1},{1,0},{2,3},{3,2},{4,5},{5,4},{6,7},{7,6},{8,9},{9,8},{10,11... | collective-permute-start | bytes 516104 | tf_op jit(solution)/shard_map/ppermute | solution.py:270
  10.4 4.6 %collective-permute-start.4 = (bf16[168,512]{1,0:T(8,128)(2,1)S(1)}, bf16[168,512]{1,0:T(8,128)(2,1)S(1)}, u32[]{:S(2)}, u32[]{:S(2)}) collective-permute-start(bf16[168,512]{1,0:T(8,128)(2,1)S(1)} %broadcast_select_fusion.1), channel_id=1, source_target_pairs={{2,0},{0,2},{6,4},{4,6},{10,8},{8,10},{14,12},{12,14},{5,1},{7,3},... | collective-permute-start | bytes 516104 | tf_op jit(solution)/shard_map/ppermute | solution.py:277
  11.5 8.5 %collective-permute-start.3 = (bf16[168,512]{1,0:T(8,128)(2,1)S(1)}, bf16[168,512]{1,0:T(8,128)(2,1)S(1)}, u32[]{:S(2)}, u32[]{:S(2)}) collective-permute-start(bf16[168,512]{1,0:T(8,128)(2,1)S(1)} %broadcast_select_fusion), channel_id=1, source_target_pairs={{4,0},{6,2},{0,4},{2,6},{12,8},{14,10},{8,12},{10,14},{7,1},{5,3},... | collective-permute-start | bytes 516104 | tf_op jit(solution)/shard_map/ppermute | solution.py:277
  15.1 5.0 %collective-permute-start.6 = (bf16[168,512]{1,0:T(8,128)(2,1)S(1)}, bf16[168,512]{1,0:T(8,128)(2,1)S(1)}, u32[]{:S(2)}, u32[]{:S(2)}) collective-permute-start(bf16[168,512]{1,0:T(8,128)(2,1)S(1)} %collective-permute-done.4.refs_9_), channel_id=1, source_target_pairs={{0,1},{1,0},{2,3},{3,2},{4,5},{5,4},{6,7},{7,6},{8,9},{9,8},{10,11... | collective-permute-start | bytes 516104 | tf_op jit(solution)/shard_map/ppermute | solution.py:270
  20.0 1.5 %collective-permute-start.7 = (bf16[168,512]{1,0:T(8,128)(2,1)S(1)}, bf16[168,512]{1,0:T(8,128)(2,1)S(1)}, u32[]{:S(2)}, u32[]{:S(2)}) collective-permute-start(bf16[168,512]{1,0:T(8,128)(2,1)S(1)} %collective-permute-done.3.refs_11_), channel_id=1, source_target_pairs={{0,1},{1,0},{2,3},{3,2},{4,5},{5,4},{6,7},{7,6},{8,9},{9,8},{10,11... | collective-permute-start | bytes 516104 | tf_op jit(solution)/shard_map/ppermute | solution.py:270

commit v7 on v6

--- a/solution.py
+++ b/solution.py
@@ -277,7 +277,7 @@
     return lax.ppermute(x, ("trade", "path"), pairs)
 
 
-LAYOUT = ((0, 4, 2, 1, 5, 3, 6, 7), (0, 2, 4, 1, 3, 5, 7, 6))
+LAYOUT = ((0, 4, 2, 1, 5, 3, 7, 6), (0, 2, 4, 1, 3, 5, 6, 7))
 EITHER = 3
 
 
@@ -327,7 +327,7 @@
     first_other = swap_cores(first)
     _, first_other = lax.optimization_barrier((sent, first_other))
     opposite = jnp.where(core == 0, first, first_other)
-    third = fetch(opposite, owners, 2, 3)
+    third = fetch(opposite, owners, 3, 2)
     present = (swap_cores(beside), beside, payload, first, first_other)
     early_trades = trades // 2 // BLOCK * BLOCK
     groups = owners * cpties

time: 28.2 us -> 28.2 us (level)
  the two profiles are of different devices: /device:TPU:27 before, /device:TPU:0 now
where the time goes in v7:
time: 28.2 us; the launch traced here: 28 us
  Pallas kernels  12.3 us (44%)
  starting transfers between devices  9.56 us (34%)
  waiting for transfers between devices  5.45 us (19%)
  between operations  0.69 us (2%)
    ppermute x4, starting transfers between devices, fetch(): return lax.ppermute(x, ('trade', 'path'), pairs)  8.68 us
    pallas_call x1, Pallas kernels, gather_body(): pl.pallas_call(late, out_shape=[jax.ShapeDtypeStruct((cpties, paths), F32...  6.55 us
    ppermute x4, waiting for transfers between devices, fetch(): return lax.ppermute(x, ('trade', 'path'), pairs)  4.04 us
    pallas_call x1, Pallas kernels, gather_body(): pl.pallas_call(early, out_shape=[jax.ShapeDtypeStruct((paths, early_trade...  2.58 us
    pallas_call x1, Pallas kernels, gather_body(): pl.pallas_call(middle, out_shape=[jax.ShapeDtypeStruct((paths, middle_tra...  2.16 us
    ppermute x4, waiting for transfers between devices, swap_cores(): return lax.ppermute(x, 'path', [(0, 1), (1, 0)])  1.41 us
    pallas_call x1, Pallas kernels, gather_body(): pl.pallas_call(pack, out_shape=jax.ShapeDtypeStruct((per + META_ROWS, wid...  1 us
    ppermute x4, starting transfers between devices, swap_cores(): return lax.ppermute(x, 'path', [(0, 1), (1, 0)])  0.87 us
  transfers between devices with their start and end apart: 8, of which 3 were waited for; matrix products, arithmetic and copies ran while one was open for 0% of the time, Pallas kernels for 17%

profile of v7, /device:TPU:0, one launch (start us, length us, event | category | flops | bytes accessed | tf_op | source)
XLA Modules:
  0.0 28.0 jit_solution(15619223511844521888)
XLA Ops:
  0.6 1.0 %shard_map.86.refs_5_.refs_6_ = bf16[168,512]{1,0:T(8,128)(2,1)S(1)} custom-call(s32[1,160]{1,0:T(1,128)} %bitcast.4, s32[1,160]{1,0:T(1,128)} %bitcast.5, f32[1,16]{1,0:T(1,128)} %bitcast.6, bf16[160,512]{1,0:T(8,128)(2,1)} %refs_3_.1), custom_call_target="tpu_custom_call" | custom-call | tf_op jit(solution)/shard_map/pallas_call | solution.py:303
  1.6 4.1 %collective-permute-start = (bf16[168,512]{1,0:T(8,128)(2,1)S(1)}, bf16[168,512]{1,0:T(8,128)(2,1)S(1)}, u32[]{:S(2)}, u32[]{:S(2)}) collective-permute-start(bf16[168,512]{1,0:T(8,128)(2,1)S(1)} %shard_map.86.refs_5_.refs_6_), channel_id=1, source_target_pairs={{8,0},{10,2},{12,4},{14,6},{0,8},{2,10},{4,12},{6,14},{5,1},{7,3},... | collective-permute-start | bytes 516104 | tf_op jit(solution)/shard_map/ppermute | solution.py:277
  5.7 0.7 %collective-permute-start.1 = (bf16[168,512]{1,0:T(8,128)(2,1)S(1)}, bf16[168,512]{1,0:T(8,128)(2,1)S(1)}, u32[]{:S(2)}, u32[]{:S(2)}) collective-permute-start(bf16[168,512]{1,0:T(8,128)(2,1)S(1)} %shard_map.86.refs_5_.refs_6_), channel_id=1, source_target_pairs={{0,0},{2,2},{4,4},{6,6},{8,8},{10,10},{12,12},{14,14},{3,1},{1,3},... | collective-permute-start | bytes 516104 | tf_op jit(solution)/shard_map/ppermute | solution.py:277
  6.4 3.2 %collective-permute-done.refs_6_.refs_7_ = bf16[168,512]{1,0:T(8,128)(2,1)S(1)} collective-permute-done((bf16[168,512]{1,0:T(8,128)(2,1)S(1)}, bf16[168,512]{1,0:T(8,128)(2,1)S(1)}, u32[]{:S(2)}, u32[]{:S(2)}) %collective-permute-start) | collective-permute-done | bytes 172064 | tf_op jit(solution)/shard_map/ppermute | solution.py:277
  9.6 0.0 collective-permute-done.1.refs_4_.refs_5_
  9.6 0.8 %collective-permute-start.2 = (bf16[168,512]{1,0:T(8,128)(2,1)S(1)}, bf16[168,512]{1,0:T(8,128)(2,1)S(1)}, u32[]{:S(2)}, u32[]{:S(2)}) collective-permute-start(bf16[168,512]{1,0:T(8,128)(2,1)S(1)} %collective-permute-done.refs_6_.refs_7_), channel_id=1, source_target_pairs={{0,1},{1,0},{2,3},{3,2},{4,5},{5,4},{6,7},{7,6},{8,9},{9,8},{10,11... | collective-permute-start | bytes 516104 | tf_op jit(solution)/shard_map/ppermute | solution.py:270
  10.4 0.0 collective-permute-start.5
  10.4 1.9 %collective-permute-start.4 = (bf16[168,512]{1,0:T(8,128)(2,1)S(1)}, bf16[168,512]{1,0:T(8,128)(2,1)S(1)}, u32[]{:S(2)}, u32[]{:S(2)}) collective-permute-start(bf16[168,512]{1,0:T(8,128)(2,1)S(1)} %broadcast_select_fusion.1), channel_id=1, source_target_pairs={{2,0},{0,2},{6,4},{4,6},{10,8},{8,10},{14,12},{12,14},{5,1},{7,3},... | collective-permute-start | bytes 516104 | tf_op jit(solution)/shard_map/ppermute | solution.py:277
  12.4 0.0 collective-permute-done.2.refs_7_.refs_8_
  12.4 2.0 %collective-permute-start.3 = (bf16[168,512]{1,0:T(8,128)(2,1)S(1)}, bf16[168,512]{1,0:T(8,128)(2,1)S(1)}, u32[]{:S(2)}, u32[]{:S(2)}) collective-permute-start(bf16[168,512]{1,0:T(8,128)(2,1)S(1)} %broadcast_select_fusion), channel_id=1, source_target_pairs={{6,0},{4,2},{2,4},{0,6},{14,8},{12,10},{10,12},{8,14},{5,1},{7,3},... | collective-permute-start | bytes 516104 | tf_op jit(solution)/shard_map/ppermute | solution.py:277
  14.4 0.0 collective-permute-done.5.refs_3_.refs_4_
  14.4 2.6 %shard_map.87 = (bf16[512,512]{1,0:T(8,128)(2,1)S(1)}, f32[512,512]{1,0:T(8,128)S(1)}, bf16[256,128]{1,0:T(8,128)(2,1)S(1)}, bf16[512,512]{1,0:T(8,128)(2,1)S(1)}) custom-call(bf16[512,512]{1,0:T(8,128)(2,1)} %refs_0_.1, f32[1,128]{1,0:T(1,128)} %bitcast.7, f32[128,128]{1,0:T(8,128)} %refs_2_.1, bf16[168,512]{1,0:T(8,128)(2,1)S(1)} %collective-permute-done.5.refs_3_.refs_4_, ...), custom_call_target="tpu_custom_call" | custom-call | flops 2000000000 | bytes 4000000 | tf_op jit(solution)/shard_map/pallas_call | solution.py:338
  17.0 0.0 collective-permute-done.4.refs_9_
  17.0 0.1 collective-permute-start.6
  17.1 2.2 %shard_map.88 = (bf16[512,768]{1,0:T(8,128)(2,1)S(1)}, f32[512,768]{1,0:T(8,128)S(1)}) custom-call(bf16[512,512]{1,0:T(8,128)(2,1)S(1)} %get-tuple-element.26.refs_0_, f32[512,512]{1,0:T(8,128)S(1)} %get-tuple-element.27.refs_1_, bf16[256,128]{1,0:T(8,128)(2,1)S(1)} %get-tuple-element.28.refs_2_, bf16[512,512]{1,0:T(8,128)(2,1)S(1)} %get-tuple-element.29.refs_3_, ...), custom_call_target="tpu_custom_call" | custom-call | flops 1000 | bytes 1000 | tf_op jit(solution)/shard_map/pallas_call | solution.py:374
  19.2 0.8 %collective-permute-done.3.refs_11_ = bf16[168,512]{1,0:T(8,128)(2,1)S(1)} collective-permute-done((bf16[168,512]{1,0:T(8,128)(2,1)S(1)}, bf16[168,512]{1,0:T(8,128)(2,1)S(1)}, u32[]{:S(2)}, u32[]{:S(2)}) %collective-permute-start.3) | collective-permute-done | bytes 172064 | tf_op jit(solution)/shard_map/ppermute | solution.py:277
  20.1 0.0 collective-permute-start.7
  20.1 0.0 collective-permute-done.6.refs_10_
  20.1 1.4 %collective-permute-done.7.refs_12_ = bf16[168,512]{1,0:T(8,128)(2,1)S(1)} collective-permute-done((bf16[168,512]{1,0:T(8,128)(2,1)S(1)}, bf16[168,512]{1,0:T(8,128)(2,1)S(1)}, u32[]{:S(2)}, u32[]{:S(2)}) %collective-permute-start.7) | collective-permute-done | bytes 172064 | tf_op jit(solution)/shard_map/ppermute | solution.py:270
  21.5 6.6 %shard_map.89 = (f32[16,512]{1,0:T(8,128)}, bf16[512,512]{1,0:T(8,128)(2,1)}) custom-call(bf16[512,768]{1,0:T(8,128)(2,1)S(1)} %get-tuple-element.33.refs_0_, f32[512,768]{1,0:T(8,128)S(1)} %get-tuple-element.34.refs_1_, bf16[256,128]{1,0:T(8,128)(2,1)S(1)} %get-tuple-element.28.refs_2_, bf16[512,512]{1,0:T(8,128)(2,1)S(1)} %get-tuple-element.29.refs_3_, ...), custom_call_target="tpu_custom_call" | custom-call | tf_op jit(solution)/shard_map/pallas_call | solution.py:399
  (2 shorter events, 0.0 us)
Async XLA Ops:
  1.6 8.0 %collective-permute-start = (bf16[168,512]{1,0:T(8,128)(2,1)S(1)}, bf16[168,512]{1,0:T(8,128)(2,1)S(1)}, u32[]{:S(2)}, u32[]{:S(2)}) collective-permute-start(bf16[168,512]{1,0:T(8,128)(2,1)S(1)} %shard_map.86.refs_5_.refs_6_), channel_id=1, source_target_pairs={{8,0},{10,2},{12,4},{14,6},{0,8},{2,10},{4,12},{6,14},{5,1},{7,3},... | collective-permute-start | bytes 516104 | tf_op jit(solution)/shard_map/ppermute | solution.py:277
  5.7 3.9 %collective-permute-start.1 = (bf16[168,512]{1,0:T(8,128)(2,1)S(1)}, bf16[168,512]{1,0:T(8,128)(2,1)S(1)}, u32[]{:S(2)}, u32[]{:S(2)}) collective-permute-start(bf16[168,512]{1,0:T(8,128)(2,1)S(1)} %shard_map.86.refs_5_.refs_6_), channel_id=1, source_target_pairs={{0,0},{2,2},{4,4},{6,6},{8,8},{10,10},{12,12},{14,14},{3,1},{1,3},... | collective-permute-start | bytes 516104 | tf_op jit(solution)/shard_map/ppermute | solution.py:277
  9.6 2.8 %collective-permute-start.2 = (bf16[168,512]{1,0:T(8,128)(2,1)S(1)}, bf16[168,512]{1,0:T(8,128)(2,1)S(1)}, u32[]{:S(2)}, u32[]{:S(2)}) collective-permute-start(bf16[168,512]{1,0:T(8,128)(2,1)S(1)} %collective-permute-done.refs_6_.refs_7_), channel_id=1, source_target_pairs={{0,1},{1,0},{2,3},{3,2},{4,5},{5,4},{6,7},{7,6},{8,9},{9,8},{10,11... | collective-permute-start | bytes 516104 | tf_op jit(solution)/shard_map/ppermute | solution.py:270
  10.4 4.0 %collective-permute-start.5 = (bf16[168,512]{1,0:T(8,128)(2,1)S(1)}, bf16[168,512]{1,0:T(8,128)(2,1)S(1)}, u32[]{:S(2)}, u32[]{:S(2)}) collective-permute-start(bf16[168,512]{1,0:T(8,128)(2,1)S(1)} %collective-permute-done.1.refs_4_.refs_5_), channel_id=1, source_target_pairs={{0,1},{1,0},{2,3},{3,2},{4,5},{5,4},{6,7},{7,6},{8,9},{9,8},{10,11... | collective-permute-start | bytes 516104 | tf_op jit(solution)/shard_map/ppermute | solution.py:270
  10.4 6.5 %collective-permute-start.4 = (bf16[168,512]{1,0:T(8,128)(2,1)S(1)}, bf16[168,512]{1,0:T(8,128)(2,1)S(1)}, u32[]{:S(2)}, u32[]{:S(2)}) collective-permute-start(bf16[168,512]{1,0:T(8,128)(2,1)S(1)} %broadcast_select_fusion.1), channel_id=1, source_target_pairs={{2,0},{0,2},{6,4},{4,6},{10,8},{8,10},{14,12},{12,14},{5,1},{7,3},... | collective-permute-start | bytes 516104 | tf_op jit(solution)/shard_map/ppermute | solution.py:277
  12.4 7.7 %collective-permute-start.3 = (bf16[168,512]{1,0:T(8,128)(2,1)S(1)}, bf16[168,512]{1,0:T(8,128)(2,1)S(1)}, u32[]{:S(2)}, u32[]{:S(2)}) collective-permute-start(bf16[168,512]{1,0:T(8,128)(2,1)S(1)} %broadcast_select_fusion), channel_id=1, source_target_pairs={{6,0},{4,2},{2,4},{0,6},{14,8},{12,10},{10,12},{8,14},{5,1},{7,3},... | collective-permute-start | bytes 516104 | tf_op jit(solution)/shard_map/ppermute | solution.py:277
  17.0 3.1 %collective-permute-start.6 = (bf16[168,512]{1,0:T(8,128)(2,1)S(1)}, bf16[168,512]{1,0:T(8,128)(2,1)S(1)}, u32[]{:S(2)}, u32[]{:S(2)}) collective-permute-start(bf16[168,512]{1,0:T(8,128)(2,1)S(1)} %collective-permute-done.4.refs_9_), channel_id=1, source_target_pairs={{0,1},{1,0},{2,3},{3,2},{4,5},{5,4},{6,7},{7,6},{8,9},{9,8},{10,11... | collective-permute-start | bytes 516104 | tf_op jit(solution)/shard_map/ppermute | solution.py:270
  20.1 1.4 %collective-permute-start.7 = (bf16[168,512]{1,0:T(8,128)(2,1)S(1)}, bf16[168,512]{1,0:T(8,128)(2,1)S(1)}, u32[]{:S(2)}, u32[]{:S(2)}) collective-permute-start(bf16[168,512]{1,0:T(8,128)(2,1)S(1)} %collective-permute-done.3.refs_11_), channel_id=1, source_target_pairs={{0,1},{1,0},{2,3},{3,2},{4,5},{5,4},{6,7},{7,6},{8,9},{9,8},{10,11... | collective-permute-start | bytes 516104 | tf_op jit(solution)/shard_map/ppermute | solution.py:270
